TPU v7x, 1024 devices: a whole 4x4x32 slice. The times are simulated.
1024 devices in a mesh: ctx: 128 (over y, z), chan: 8 (over x, core).
Axes of the slice: x: 4, y: 4, z: 32, core: 2. Of those that a mesh axis runs over, the one named last changes fastest.
Arguments:
- features: bfloat16 [32768, 3, 8192], P('ctx', None, 'chan'), may hold values from -29 to 29
- short_taps: float32 [3, 3, 8192], P(None, None, 'chan'), may hold values from -3 to 3
- decay_rate: float32 [16, 8192], P(None, 'chan'), may hold values from 1.5258789e-05 to 0.0333333333
- residue: float32 [16, 8192], P(None, 'chan'), may hold values from -1.5 to 1.5
- skip_gain: float32 [8192], P('chan'), may hold values from -4 to 4
- norm_gain: float32 [8192], P('chan'), may hold values from 0.5 to 1.5
- contig_lengths: int32 [4], replicated, may hold values from 1 to 16384, 32768 in all
Outputs:
- normed: bfloat16 [32768, 8192], P('ctx', 'chan')
Inputs may be any that keep to these rules, and one draw needn't show every extreme that they name: `contig_lengths`: the lengths sum to 32768 and the longest is exactly 16384.
All inputs are finite; a program needn't handle non-finite values.
Results may differ from a plain program's by a relative error of at most 0.0024.
Values may be sent and summed in bfloat16 or wider, within the bound.
No kernel may reach another device: no remote copies, remote signals or barrier semaphores. Data moves between devices by JAX's collectives and lax.ppermute only.
A program may use at most 64 MiB of HBM per device.

v0:
```python
import jax
import jax.numpy as jnp
from jax import lax
from jax.sharding import PartitionSpec as P

D = 8192


eps_norm = 1e-05


def passed_along(value, axis, by):
    count = lax.axis_size(axis)
    pairs = [(i, i + by) for i in range(count) if 0 <= i + by < count]
    return lax.ppermute(value, axis, pairs)


def carried_in(value, axis, join, neutral):
    count, mine = (lax.axis_size(axis), lax.axis_index(axis))
    pieces = jax.tree.map(lambda part: lax.all_gather(part, axis), value)
    subtotal = jax.tree.map(
        lambda part, zero: jnp.full_like(part, 0) + jnp.asarray(zero, part.dtype), value, neutral
    )

    def turn(position, subtotal):
        longer = join(subtotal, jax.tree.map(lambda part: part[position], pieces))
        return jax.tree.map(lambda new, old: jnp.where(position < mine, new, old), longer, subtotal)

    return lax.fori_loop(0, count - 1, turn, subtotal)


def segment_of(places, bounds):
    return jnp.sum((places[:, None] >= bounds[None, :]).astype(jnp.int32), axis=1)


def shards(features, short_taps, decay_rate, residue, skip_gain, norm_gain, contig_lengths):
    tok_rows = features.shape[0]
    channels = features.shape[2]
    poles = decay_rate.shape[0]
    anchor = lax.axis_index("ctx") * tok_rows
    bounds = jnp.cumsum(contig_lengths)[:-1]
    places = anchor + jnp.arange(tok_rows, dtype=jnp.int32)
    segment = segment_of(places, bounds)
    keep_one = ((segment_of(places - 1, bounds) == segment) & (places >= 1)).astype(jnp.float32)
    keep_two = ((segment_of(places - 2, bounds) == segment) & (places >= 2)).astype(jnp.float32)
    before = segment_of(jnp.reshape(anchor - 1, (1,)), bounds)[0]
    joined = ((segment == before) & (anchor >= 1)).astype(jnp.float32)
    edge_rows = passed_along(features[tok_rows - 2 :], "ctx", 1)
    extended = jnp.concatenate([edge_rows, features], axis=0).astype(jnp.float32)
    mixed_rows = (
        short_taps[0] * extended[2:]
        + short_taps[1] * extended[1:-1] * keep_one[:, None, None]
        + short_taps[2] * extended[:-2] * keep_two[:, None, None]
    )
    query_part = mixed_rows[:, 0]
    product = mixed_rows[:, 1] * mixed_rows[:, 2]
    input_scale = jnp.sqrt(1.0 - jnp.exp(-2.0 * decay_rate))
    block_rows = min(tok_rows, 128)
    steps_in = jnp.arange(block_rows, dtype=jnp.float32)
    carries = jnp.zeros((poles, channels), jnp.float32)
    pieces = []
    for block_index in range(tok_rows // block_rows):
        first_row = block_index * block_rows
        seg_block = segment[first_row : first_row + block_rows]
        lower_mask = (
            (steps_in[None, :] <= steps_in[:, None]) & (seg_block[:, None] == seg_block[None, :])
        ).astype(jnp.float32)
        if first_row > 0:
            head_block = (seg_block == segment[first_row - 1]).astype(jnp.float32)
        else:
            head_block = jnp.zeros((block_rows,), jnp.float32)
        drive_rows = product[first_row : first_row + block_rows]

        def one_mode(mode_index, carry):
            total_rows, states = carry
            rate_row = decay_rate[mode_index]
            scaled = jnp.exp(rate_row[None, :] * steps_in[:, None]) * (
                drive_rows * input_scale[mode_index][None, :]
            )
            summed = jnp.dot(
                lower_mask,
                scaled,
                precision=lax.Precision.HIGHEST,
                preferred_element_type=jnp.float32,
            )
            state_rows = (
                jnp.exp(-rate_row[None, :] * steps_in[:, None]) * summed
                + jnp.exp(-rate_row[None, :] * (steps_in[:, None] + 1.0))
                * states[mode_index][None, :]
                * head_block[:, None]
            )
            total_rows = total_rows + residue[mode_index][None, :] * state_rows
            states = states.at[mode_index].set(state_rows[block_rows - 1])
            return (total_rows, states)

        block_sum, carries = lax.fori_loop(
            0, poles, one_mode, (jnp.zeros((block_rows, channels), jnp.float32), carries)
        )
        pieces.append(block_sum)
    local_filtered = jnp.concatenate(pieces, axis=0)
    through = jnp.exp(-decay_rate * tok_rows) * joined[tok_rows - 1]

    def chain_factor(earlier, later):
        return (earlier[0] * later[0], later[0] * earlier[1] + later[1])

    arrived = carried_in(
        (through, carries), "ctx", chain_factor, (jnp.ones_like(through), jnp.zeros_like(carries))
    )[1]
    offsets = jnp.arange(tok_rows, dtype=jnp.float32) + 1.0
    weight_in = residue * arrived
    incoming = (
        jnp.sum(
            jnp.exp(-decay_rate[None, :, :] * offsets[:, None, None]) * weight_in[None, :, :],
            axis=1,
        )
        * joined[:, None]
    )
    response = query_part * (local_filtered + incoming + skip_gain[None, :] * product)
    squares = lax.psum(jnp.sum(response * response, axis=1), "chan")
    scale_rows = lax.rsqrt(squares / D + eps_norm)
    return (response * scale_rows[:, None] * norm_gain[None, :]).astype(jnp.bfloat16)


def solution(mesh):
    placed = (
        P("ctx", None, "chan"),
        P(None, None, "chan"),
        P(None, "chan"),
        P(None, "chan"),
        P("chan"),
        P("chan"),
        P(),
    )
    return jax.shard_map(
        shards, mesh=mesh, in_specs=placed, out_specs=P("ctx", "chan"), check_vma=False
    )
```

profile of v0, /device:TPU:1, one launch (start us, length us, event | category | flops | bytes accessed | tf_op | source)
XLA Modules:
  0.0 734.5 jit_solution(6623158195967519469)
XLA Ops:
  7.4 4.4 collective-permute-start
  23.3 83.5 %while.51 = (s32[]{:T(128)}, f32[128,1024]{1,0:T(8,128)}, f32[16,1024]{1,0:T(8,128)S(1)}, f32[16,1024]{1,0:T(8,128)S(1)}, f32[16,1024]{1,0:T(8,128)}, /*index=5*...) while((s32[]{:T(128)}, f32[128,1024]{1,0:T(8,128)}, ...), condition=%wide.region_6.7_spmd.clone.clone, body=%wide.region_4.6_spmd.clone.clone.sunk | while | flops 202967184 | bytes 2176669 | solution.py:96
  29.2 2.9 select_add_fusion.4
  34.4 2.9 select_add_fusion.4
  39.6 2.9 select_add_fusion.4
  44.8 2.9 select_add_fusion.4
  50.1 2.9 select_add_fusion.4
  55.3 2.9 select_add_fusion.4
  60.5 2.9 select_add_fusion.4
  65.7 2.9 select_add_fusion.4
  71.0 2.9 select_add_fusion.4
  76.2 2.9 select_add_fusion.4
  81.4 2.9 select_add_fusion.4
  86.7 2.9 select_add_fusion.4
  102.3 2.9 select_add_fusion.4
  106.7 83.7 %while.52 = (s32[]{:T(128)}, f32[128,1024]{1,0:T(8,128)}, f32[16,1024]{1,0:T(8,128)S(1)}, f32[16,1024]{1,0:T(8,128)S(1)}, f32[16,1024]{1,0:T(8,128)}, /*index=5*...) while((s32[]{:T(128)}, f32[128,1024]{1,0:T(8,128)}, ...), condition=%wide.region_9.10_spmd.clone.clone, body=%wide.region_7.9_spmd.clone.clone.sunk | while | flops 202967184 | bytes 2177189 | solution.py:96
  112.6 2.9 select_add_fusion.5
  117.9 2.9 select_add_fusion.5
  128.4 2.9 select_add_fusion.5
  191.1 100.1 %all-gather.5.cloned.1.call-done = f32[2048,1024]{1,0:T(8,128)} async-done(((f32[16,1024]{1,0:T(8,128)}), f32[2048,1024]{1,0:T(8,128)}) %all-gather.5.cloned.1.call-update) | async-done | bytes 8388624 | tf_op jit(solution)/shard_map/all_gather | solution.py:20
  291.2 278.4 %all-gather.7.cloned.1.call-done = f32[2048,1024]{1,0:T(8,128)} async-done(((f32[16,1024]{1,0:T(8,128)}), f32[2048,1024]{1,0:T(8,128)}) %all-gather.7.cloned.1.call-update) | async-done | bytes 8388624 | tf_op jit(solution)/shard_map/all_gather | solution.py:20
  569.6 119.0 %while.50 = (s32[]{:T(128)}, f32[16,1024]{1,0:T(8,128)S(1)}, s32[]{:T(128)}, f32[128,16,1024]{2,1,0:T(8,128)}, f32[128,16,1024]{2,1,0:T(8,128)}, /*index=5*/s32[]{:T(128)}, s32[]{:T(128)}) while((s32[]{:T(128)}, f32[16,1024]{1,0:T(8,128)S(1)}, s32[]{:T(128)}, f32[128,16,1024]{2,1,0:T(8,128)}, f32[128,16,1024]{2,1,0:T(8,128)}, ...), condition=%wide.region_12.13_spmd.clone, body=%wide.region_11.12_spmd.clone.sunk | while | flops 65540 | bytes 262245 | solution.py:29
  688.7 5.5 multiply_reduce_fusion
  695.6 29.9 %psum.7 = f32[256]{0:T(256)S(1)} all-reduce(f32[256]{0:T(256)S(1)} %get-tuple-element.669), channel_id=1, replica_groups=mesh['ctx'=128,'chan'=8] {'chan'}, use_global_device_ids=true, to_apply=%region_15.16 | all-reduce | flops 256 | bytes 2048 | tf_op jit(solution)/shard_map/psum | solution.py:119
  (380 shorter events, 251.8 us)
Async XLA Ops:
  6.5 284.7 %all-gather.5.cloned.1.call-start = ((), (), s32[]{:S(2)}) async-start(), calls=%async_computation | async-start | bytes 8454144 | tf_op jit(solution)/shard_map/all_gather | solution.py:20
  7.4 11.5 %collective-permute-start = (bf16[2,3,1024]{2,0,1:T(2,128)(2,1)S(1)}, bf16[2,3,1024]{2,0,1:T(2,128)(2,1)S(1)}, u32[]{:S(2)}, u32[]{:S(2)}) collective-permute-start(bf16[2,3,1024]{2,0,1:T(2,128)(2,1)S(1)} %slice.125), channel_id=1, source_target_pairs={{0,8},{8,16},{16,24},{24,32},{32,40},{40,48},{48,56},{56,64},{64,7... | collective-permute-start | bytes 36872 | tf_op jit(solution)/shard_map/ppermute | solution.py:15
  16.7 552.9 %all-gather.7.cloned.1.call-start = ((), (), s32[]{:S(2)}) async-start(), calls=%async_computation.1 | async-start | bytes 8454144 | tf_op jit(solution)/shard_map/all_gather | solution.py:20
  21.9 1.3 copy-start.3
  21.9 1.3 copy-start.4
  190.5 0.6 copy-start.2
  688.6 5.5 copy-start
  688.7 5.5 copy-start.1
  688.7 5.5 copy-start.5
  694.2 31.3 %copy-start.6 = (f32[1024]{0:T(1024)S(1)}, f32[1024]{0:T(1024)}, u32[]{:S(2)}) copy-start(f32[1024]{0:T(1024)} %param.22) | copy-start | bytes 12292
Sparse Core Ops, SparseCore 0:
  16.8 274.3 all-gather.4
  295.3 274.2 all-gather.6
where the time goes:
time: 744 us; the launch traced here: 735 us
  waiting for transfers between devices  378 us (51%)
  other arithmetic  203 us (27%)
  matrix products  92.4 us (12%)
  blocking collectives  29.9 us (4%)
  between operations  13.7 us (2%)
  local copies, waits for them, and re-layouts  8.59 us (1%)
    all_gather x2, waiting for transfers between devices, carried_in(): pieces = jax.tree.map(lambda part: lax.all_gather(part, axis), value)  378 us
    select_n x127, other arithmetic, turn(): jnp.where(position < mine, new, old)  116 us
    dot_general x32, matrix products, one_mode(): jnp.dot(lower_mask, scaled, precision=lax.Precision.HIGHEST, preferred_el...  92.4 us
    another operation x65, other arithmetic  44.9 us
    psum x1, blocking collectives, shards(): squares = lax.psum(jnp.sum(response * response, axis=1), 'chan')  29.9 us
    neg x32, other arithmetic, one_mode(): -rate_row[None, :] * steps_in[:, None]  24.8 us
  transfers between devices with their start and end apart: 3, of which 2 were waited for; matrix products, arithmetic and copies ran while one was open for 24% of the time, Pallas kernels for 0%

commit v1 on v0

v1 whole, which is shorter than its diff:
```python
import functools

import jax
import jax.numpy as jnp
from jax import lax
from jax.experimental import pallas as pl
from jax.experimental.pallas import tpu as pltpu
from jax.sharding import PartitionSpec as P

D = 8192
eps_norm = 1e-05
CHUNK = 16
PAD = 8
HIGH = lax.Precision.HIGHEST


def starts_of(lengths, anchor):
    one = lengths[0]
    two = one + lengths[1]
    three = two + lengths[2]
    return [-anchor, one - anchor, two - anchor, three - anchor]


def hits(starts, low, high):
    found = (starts[0] >= low) & (starts[0] < high)
    for start in starts[1:]:
        found = found | ((start >= low) & (start < high))
    return found


def as_tiles(rows, ref, sub, lanes):
    for tile in range(sub):
        rows[pl.ds(tile * ref.shape[0], ref.shape[0]), :] = ref[:, tile * lanes : (tile + 1) * lanes]


def row_tile(rows, row, count, sub):
    return rows[pl.ds(row, sub, stride=count), :]


def first_pass(lengths, x_ref, edge_ref, taps_ref, rate_ref, state_ref, product_ref, query_ref,
               spread, rate_rows, taps_rows):
    toks, sub, lanes = product_ref.shape
    poles = rate_ref.shape[0]
    pitch = toks + PAD
    anchor = lax.axis_index("ctx") * toks
    starts = starts_of(lengths, anchor)
    for part in range(3):
        for tile in range(sub):
            cols = slice(tile * lanes, (tile + 1) * lanes)
            spread[part, pl.ds(tile * pitch + PAD, toks), :] = x_ref[part, :, cols].astype(jnp.float32)
            spread[part, pl.ds(tile * pitch + PAD - 2, 2), :] = edge_ref[part, :, cols].astype(jnp.float32)
    as_tiles(rate_rows, rate_ref, sub, lanes)
    for tap in range(3):
        for part in range(3):
            for tile in range(sub):
                taps_rows[tap * 3 + part, pl.ds(tile, 1), :] = taps_ref[
                    tap, pl.ds(part, 1), tile * lanes : (tile + 1) * lanes
                ]
    fades = [jnp.exp(-row_tile(rate_rows, n, poles, sub)) for n in range(poles)]
    state_ref[...] = jnp.zeros_like(state_ref)

    def token_rows(t):
        return [spread[part, pl.ds(t + PAD, sub, stride=pitch), :] for part in range(3)]

    def chunk(index, _):
        base = index * CHUNK

        def steps(masked):
            states = [state_ref[n] for n in range(poles)]
            two, one = token_rows(base - 2), token_rows(base - 1)
            for i in range(CHUNK):
                t = base + i
                now = token_rows(t)
                if masked:
                    link_one = jnp.where(hits(starts, t, t + 1), 0.0, 1.0).astype(jnp.float32)
                    link_two = jnp.where(hits(starts, t - 1, t + 1), 0.0, 1.0).astype(jnp.float32)
                mixed = []
                for part in range(3):
                    term_one = taps_rows[3 + part] * one[part]
                    term_two = taps_rows[6 + part] * two[part]
                    if masked:
                        term_one, term_two = term_one * link_one, term_two * link_two
                    mixed.append(taps_rows[part] * now[part] + term_one + term_two)
                product = mixed[1] * mixed[2]
                query_ref[t] = mixed[0]
                product_ref[t] = product
                if masked:
                    states = [s * link_one for s in states]
                states = [fades[n] * states[n] + product for n in range(poles)]
                two, one = one, now
            for n in range(poles):
                state_ref[n] = states[n]

        cut = hits(starts, base - 1, base + CHUNK)

        @pl.when(cut)
        def _():
            steps(True)

        @pl.when(jnp.logical_not(cut))
        def _():
            steps(False)

        return 0

    lax.fori_loop(0, toks // CHUNK, chunk, 0)


def scan_devices(toks, lengths, ends_ref, rate_ref, arrived_ref, rows):
    count, lanes = ends_ref.shape
    sub = rate_ref.shape[1] // lanes
    mine = lax.axis_index("ctx")
    as_tiles(rows, rate_ref, sub, lanes)
    rate = rows[pl.ds((mine % sub) * rate_ref.shape[0] + mine // sub, 1), :]
    place = lax.broadcasted_iota(jnp.int32, (count, lanes), 0)
    first = place * toks
    cut = hits(starts_of(lengths, 0), first, first + toks)
    factor = jnp.where(cut, 0.0, jnp.exp(rate * (-float(toks))))
    total = ends_ref[...]
    step = 1
    while step < count:
        total = total + factor * pltpu.roll(total, step, 0)
        factor = factor * pltpu.roll(factor, step, 0)
        step *= 2
    arrived_ref[...] = jnp.where(place == 0, 0.0, pltpu.roll(total, 1, 0))


def second_pass(lengths, arrived_ref, product_ref, query_ref, rate_ref, residue_ref, skip_ref,
                response_ref, squares_ref, spread, states_ref, rate_rows, residue_rows):
    toks, sub, lanes = product_ref.shape
    poles = rate_ref.shape[0]
    anchor = lax.axis_index("ctx") * toks
    starts = starts_of(lengths, anchor)
    as_tiles(rate_rows, rate_ref, sub, lanes)
    as_tiles(residue_rows, residue_ref, sub, lanes)
    fades, gains = [], []
    for n in range(poles):
        rate = row_tile(rate_rows, n, poles, sub)
        fades.append(jnp.exp(-rate))
        gains.append(row_tile(residue_rows, n, poles, sub) * jnp.sqrt(1.0 - jnp.exp(-2.0 * rate)))
    skip = skip_ref[...]
    states_ref[...] = arrived_ref[...]

    def chunk(index, _):
        base = index * CHUNK

        def steps(masked):
            states = [states_ref[n] for n in range(poles)]
            for i in range(CHUNK):
                t = base + i
                product = product_ref[t]
                if masked:
                    link = jnp.where(hits(starts, t, t + 1), 0.0, 1.0).astype(jnp.float32)
                    states = [s * link for s in states]
                states = [fades[n] * states[n] + product for n in range(poles)]
                sums = [gains[n] * states[n] for n in range(poles)] + [skip * product]
                while len(sums) > 1:
                    sums = [a + b for a, b in zip(sums[::2], sums[1::2])] + (
                        [sums[-1]] if len(sums) % 2 else []
                    )
                spread[pl.ds(t, sub, stride=toks), :] = query_ref[t] * sums[0]
            for n in range(poles):
                states_ref[n] = states[n]

        cut = hits(starts, base, base + CHUNK)

        @pl.when(cut)
        def _():
            steps(True)

        @pl.when(jnp.logical_not(cut))
        def _():
            steps(False)

        return 0

    lax.fori_loop(0, toks // CHUNK, chunk, 0)
    total = jnp.zeros((toks, lanes), jnp.float32)
    for tile in range(sub):
        part = spread[pl.ds(tile * toks, toks), :]
        response_ref[:, tile * lanes : (tile + 1) * lanes] = part
        total = total + part * part
    sums = lax.dot_general(
        jnp.ones((squares_ref.shape[0], lanes), jnp.float32), total, (((1,), (1,)), ((), ())),
        precision=HIGH, preferred_element_type=jnp.float32,
    )
    halves = toks // lanes
    half = lax.broadcasted_iota(jnp.int32, squares_ref.shape, 0) % halves
    picked = sums[:, :lanes]
    for h in range(1, halves):
        picked = jnp.where(half == h, sums[:, h * lanes : (h + 1) * lanes], picked)
    squares_ref[...] = picked


def last_pass(squares_ref, response_ref, gain_ref, out_ref):
    count, lanes = squares_ref.shape
    halves = out_ref.shape[0] // lanes
    half = lax.broadcasted_iota(jnp.int32, (count, lanes), 0) % halves
    for h in range(halves):
        sums = lax.dot_general(
            squares_ref[...], (half == h).astype(jnp.float32), (((0,), (0,)), ((), ())),
            precision=HIGH, preferred_element_type=jnp.float32,
        )
        scale = lax.rsqrt(sums / D + eps_norm)
        toks = slice(h * lanes, (h + 1) * lanes)
        for tile in range(response_ref.shape[1] // lanes):
            cols = slice(tile * lanes, (tile + 1) * lanes)
            out_ref[toks, cols] = (response_ref[toks, cols] * scale * gain_ref[:, cols]).astype(jnp.bfloat16)


SCALARS = pl.BlockSpec(memory_space=pltpu.SMEM)
VECTORS = pl.BlockSpec(memory_space=pltpu.VMEM)
F32 = jnp.float32


def call(body, inputs, outputs, scratch, name):
    return pl.pallas_call(
        body,
        in_specs=[SCALARS if i is None else VECTORS for i in inputs],
        out_specs=jax.tree.map(lambda _: VECTORS, outputs),
        out_shape=outputs,
        scratch_shapes=scratch,
        compiler_params=pltpu.CompilerParams(vmem_limit_bytes=40 << 20),
        name=name,
    )


def shards(features, short_taps, decay_rate, residue, skip_gain, norm_gain, contig_lengths):
    toks, _, channels = features.shape
    poles = decay_rate.shape[0]
    lanes, sub = 128, channels // 128
    count, wide = lax.axis_size("ctx"), lax.axis_size("chan")
    tile = lambda *lead: jax.ShapeDtypeStruct((*lead, sub, lanes), F32)
    flat = lambda *dims: jax.ShapeDtypeStruct(dims, F32)
    rows = pltpu.VMEM((poles * sub, lanes), F32)
    parts = jnp.transpose(features, (1, 0, 2))
    edge = lax.ppermute(parts[:, toks - 2 :], "ctx", [(i, i + 1) for i in range(count - 1)])
    ends, product, query = call(
        first_pass, [None, 1, 1, 1, 1], (tile(poles), tile(toks), tile(toks)),
        [pltpu.VMEM((3, sub * (toks + PAD), lanes), F32), rows, pltpu.VMEM((9, sub, lanes), F32)],
        "first_pass",
    )(contig_lengths, parts, edge, short_taps, decay_rate)
    ends = lax.all_to_all(jnp.reshape(ends, (poles * sub, lanes)), "ctx", 0, 0, tiled=True)
    arrived = call(
        functools.partial(scan_devices, toks), [None, 1, 1], flat(count, lanes), [rows], "scan_devices"
    )(contig_lengths, ends, decay_rate)
    arrived = lax.all_to_all(arrived, "ctx", 0, 0, tiled=True)
    response, squares = call(
        second_pass, [None, 1, 1, 1, 1, 1, 1],
        (flat(toks, channels), flat(wide * toks // lanes, lanes)),
        [pltpu.VMEM((sub * toks, lanes), F32), pltpu.VMEM((poles, sub, lanes), F32), rows, rows],
        "second_pass",
    )(contig_lengths, jnp.reshape(arrived, (poles, sub, lanes)), product, query, decay_rate, residue,
      jnp.reshape(skip_gain, (sub, lanes)))
    squares = lax.all_to_all(squares, "chan", 0, 0, tiled=True)
    return call(
        last_pass, [1, 1, 1], jax.ShapeDtypeStruct((toks, channels), jnp.bfloat16), [], "last_pass"
    )(squares, response, jnp.reshape(norm_gain, (1, channels)))


def solution(mesh):
    placed = (
        P("ctx", None, "chan"),
        P(None, None, "chan"),
        P(None, "chan"),
        P(None, "chan"),
        P("chan"),
        P("chan"),
        P(),
    )
    return jax.shard_map(
        shards, mesh=mesh, in_specs=placed, out_specs=P("ctx", "chan"), check_vma=False
    )
```

time: 744 us -> 120 us (0.16); the launches traced: 735 us -> 120 us
  waiting for transfers between devices: 378 us -> 0.81 us
  other arithmetic: 203 us -> 0 us
  matrix products: 92.4 us -> 0 us
  blocking collectives: 29.9 us -> 101 us
  between operations: 13.7 us -> 0.04 us
  Pallas kernels: 0 us -> 8.65 us
    all_gather x2 -> x0, waiting for transfers between devices: 378 us -> none  [carried_in(): pieces = jax.tree.map(lambda part: lax.all_gather(part, axis), value)]
    select_n x127 -> x0, other arithmetic: 116 us -> none  [turn(): jnp.where(position < mine, new, old)]
    all_to_all x0 -> x3, blocking collectives: none -> 101 us  [the longest x1 58.3 us: shards(): lax.all_to_all(jnp.reshape(ends, (poles * sub, lanes)), 'ctx', 0, 0, tile...]
    dot_general x32 -> x0, matrix products: 92.4 us -> none  [one_mode(): jnp.dot(lower_mask, scaled, precision=lax.Precision.HIGHEST, preferred_el...]
    another operation x65 -> x0, other arithmetic: 44.9 us -> none
    psum x1 -> x0, blocking collectives: 29.9 us -> none  [shards(): squares = lax.psum(jnp.sum(response * response, axis=1), 'chan')]
    neg x33 -> x0, other arithmetic: 26.9 us -> none  [the longest x32 24.8 us: one_mode(): -rate_row[None, :] * steps_in[:, None]]
    pallas_call x0 -> x4, Pallas kernels: none -> 8.65 us  [the longest x1 3.68 us: shards(): call(second_pass, [None, 1, 1, 1, 1, 1, 1], (flat(toks, channels), flat(w...]
  transfers between devices with their start and end apart: 3 -> 1, of which waited for: 2 -> 1; matrix products, arithmetic and copies ran while one was open for 24% -> 0% of each run, Pallas kernels for 0% -> 0%
where the time goes in v1:
time: 120 us
  blocking collectives  101 us (84%)
  Pallas kernels  8.65 us (7%)
  local copies, waits for them, and re-layouts  4.54 us (4%)
  starting transfers between devices  4.37 us (4%)
    all_to_all x1, blocking collectives, shards(): lax.all_to_all(jnp.reshape(ends, (poles * sub, lanes)), 'ctx', 0, 0, tile...  58.3 us
    all_to_all x1, blocking collectives, shards(): arrived = lax.all_to_all(arrived, 'ctx', 0, 0, tiled=True)  30.4 us
    all_to_all x1, blocking collectives, shards(): squares = lax.all_to_all(squares, 'chan', 0, 0, tiled=True)  12.7 us
    ppermute x1, starting transfers between devices, shards(): lax.ppermute(parts[:, toks - 2:], 'ctx', [(i, i + 1) for i in range(count...  4.37 us
    unnamed x14, local copies, waits for them, and re-layouts  3.71 us
    pallas_call x1, Pallas kernels, shards(): call(second_pass, [None, 1, 1, 1, 1, 1, 1], (flat(toks, channels), flat(w...  3.68 us
    pallas_call x1, Pallas kernels, shards(): call(first_pass, [None, 1, 1, 1, 1], (tile(poles), tile(toks), tile(toks)...  3.06 us
  transfers between devices with their start and end apart: 1, of which 1 were waited for; matrix products, arithmetic and copies ran while one was open for 0% of the time, Pallas kernels for 0%

profile of v1, /device:TPU:1, one launch (start us, length us, event | category | flops | bytes accessed | tf_op | source)
XLA Modules:
  0.0 119.8 jit_solution(4943464870435961911)
XLA Ops:
  0.0 0.0 copy-start.5
  0.0 0.8 slice.4
  0.8 4.4 %collective-permute-start = (bf16[3,2,1024]{2,1,0:T(2,128)(2,1)S(1)}, bf16[3,2,1024]{2,1,0:T(2,128)(2,1)S(1)}, u32[]{:S(2)}, u32[]{:S(2)}) collective-permute-start(bf16[3,2,1024]{2,1,0:T(2,128)(2,1)S(1)} %slice.4), channel_id=1, source_target_pairs={{0,8},{8,16},{16,24},{24,32},{32,40},{40,48},{48,56},{56,64},{64,7... | collective-permute-start | bytes 36872 | tf_op jit(solution)/shard_map/ppermute | solution.py:237
  5.2 0.8 collective-permute-done.edge_ref
  6.0 0.0 copy-start
  6.0 1.4 %copy-done = bf16[256,3,1024]{2,0,1:T(8,128)(2,1)S(1)} copy-done((bf16[256,3,1024]{2,0,1:T(8,128)(2,1)S(1)}, bf16[256,3,1024]{2,0,1:T(8,128)(2,1)}, u32[]{:S(2)}) %copy-start) | copy-done | bytes 1572888
  7.4 0.0 copy-start.1
  7.4 0.8 copy-done.1
  8.3 0.0 copy-start.3
  8.3 0.8 copy-done.3
  9.1 0.0 copy-start.4
  9.1 0.7 copy-done.4
  9.7 0.0 copy-start.2
  9.7 3.1 %first_pass.1 = (f32[16,8,128]{2,1,0:T(8,128)S(1)}, f32[256,8,128]{2,1,0:T(8,128)S(1)}, f32[256,8,128]{2,1,0:T(8,128)S(1)}) custom-call(s32[4]{0:T(128)S(1)} %copy-done.4, bf16[3,256,1024]{2,1,0:T(8,128)(2,1)S(1)} %bitcast.14, bf16[3,2,1024]{2,1,0:T(2,128)(2,1)S(1)} %collective-permute-done.edge_ref, f32[3,3,1024]{2,1,0:T(4,128)S(1)} %copy-done.3, ...), custom_call_target="tpu_custom_call" | custom-call | tf_op jit(solution)/shard_map/first_pass/pallas_call | solution.py:238
  12.8 0.0 copy-start.6
  12.8 58.3 %all_to_all.31 = f32[128,1,128]{2,1,0:T(1,128)S(1)} all-to-all(f32[128,1,128]{2,1,0:T(1,128)S(1)} %bitcast.18), channel_id=1, replica_groups=mesh['ctx'=128,'chan'=8] {'ctx'}, dimensions={0} | all-to-all | bytes 131072 | tf_op jit(solution)/shard_map/all_to_all | solution.py:243
  71.1 0.7 scan_devices.1
  71.8 30.4 %all_to_all.32 = f32[128,1,128]{2,1,0:T(1,128)S(1)} all-to-all(f32[128,1,128]{2,1,0:T(1,128)S(1)} %bitcast.17), channel_id=1, replica_groups=mesh['ctx'=128,'chan'=8] {'ctx'}, dimensions={0} | all-to-all | bytes 131072 | tf_op jit(solution)/shard_map/all_to_all | solution.py:247
  102.2 0.0 copy-done.5
  102.2 0.0 copy-done.2
  102.2 3.7 %second_pass.1 = (f32[256,1024]{1,0:T(8,128)S(1)}, f32[16,128]{1,0:T(8,128)S(1)}) custom-call(s32[4]{0:T(128)S(1)} %copy-done.4, f32[16,8,128]{2,1,0:T(8,128)S(1)} %bitcast.15, f32[256,8,128]{2,1,0:T(8,128)S(1)} %get-tuple-element.11.product_ref, f32[256,8,128]{2,1,0:T(8,128)S(1)} %get-tuple-element.12.query_ref, f32[16,1024]{1,0:T(8,128)S(1)} %copy-done.1, ...), custom_call_target="tpu_custom_call" | custom-call | tf_op jit(solution)/shard_map/second_pass/pallas_call | solution.py:248
  105.9 12.7 %all_to_all.33 = f32[8,2,128]{2,1,0:T(2,128)S(1)} all-to-all(f32[8,2,128]{2,1,0:T(2,128)S(1)} %bitcast.20), channel_id=1, replica_groups=mesh['ctx'=128,'chan'=8] {'chan'}, dimensions={0} | all-to-all | bytes 16384 | tf_op jit(solution)/shard_map/all_to_all | solution.py:255
  118.6 0.0 copy-done.6
  118.6 1.2 %last_pass.1 = bf16[256,1024]{1,0:T(8,128)(2,1)} custom-call(f32[16,128]{1,0:T(8,128)S(1)} %bitcast.19, f32[256,1024]{1,0:T(8,128)S(1)} %get-tuple-element.14.response_ref, f32[1,1024]{1,0:T(1,128)S(1)} %bitcast.22), custom_call_target="tpu_custom_call" | custom-call | tf_op jit(solution)/shard_map/last_pass/pallas_call | solution.py:256
Async XLA Ops:
  0.0 102.2 %copy-start.5 = (f32[1024]{0:T(1024)S(1)}, f32[1024]{0:T(1024)}, u32[]{:S(2)}) copy-start(f32[1024]{0:T(1024)} %param.11) | copy-start | bytes 12292
  0.8 5.2 %collective-permute-start = (bf16[3,2,1024]{2,1,0:T(2,128)(2,1)S(1)}, bf16[3,2,1024]{2,1,0:T(2,128)(2,1)S(1)}, u32[]{:S(2)}, u32[]{:S(2)}) collective-permute-start(bf16[3,2,1024]{2,1,0:T(2,128)(2,1)S(1)} %slice.4), channel_id=1, source_target_pairs={{0,8},{8,16},{16,24},{24,32},{32,40},{40,48},{48,56},{56,64},{64,7... | collective-permute-start | bytes 36872 | tf_op jit(solution)/shard_map/ppermute | solution.py:237
  6.0 1.4 %copy-start = (bf16[256,3,1024]{2,0,1:T(8,128)(2,1)S(1)}, bf16[256,3,1024]{2,0,1:T(8,128)(2,1)}, u32[]{:S(2)}) copy-start(bf16[256,3,1024]{2,0,1:T(8,128)(2,1)} %param.7) | copy-start | bytes 4718596
  7.4 0.8 copy-start.1
  8.3 0.8 copy-start.3
  9.1 0.7 copy-start.4
  9.7 92.5 %copy-start.2 = (f32[16,1024]{1,0:T(8,128)S(1)}, f32[16,1024]{1,0:T(8,128)}, u32[]{:S(2)}) copy-start(f32[16,1024]{1,0:T(8,128)} %residue_ref.1) | copy-start | bytes 196612
  12.8 105.8 %copy-start.6 = (f32[1024]{0:T(1024)S(1)}, f32[1024]{0:T(1024)}, u32[]{:S(2)}) copy-start(f32[1024]{0:T(1024)} %param.12) | copy-start | bytes 12292

commit v2 on v1

v2 whole, which is shorter than its diff:
```python
import functools

import jax
import jax.numpy as jnp
from jax import lax
from jax.experimental import pallas as pl
from jax.experimental.pallas import tpu as pltpu
from jax.sharding import Mesh, PartitionSpec as P

D = 8192
eps_norm = 1e-05
CHUNK = 16
PAD = 8
PIECES = 4
CTX = ("row", "far", "near")
HIGH = lax.Precision.HIGHEST


def starts_of(lengths, anchor):
    one = lengths[0]
    two = one + lengths[1]
    three = two + lengths[2]
    return [-anchor, one - anchor, two - anchor, three - anchor]


def hits(starts, low, high):
    found = (starts[0] >= low) & (starts[0] < high)
    for start in starts[1:]:
        found = found | ((start >= low) & (start < high))
    return found


def as_tiles(rows, ref, sub, lanes):
    for tile in range(sub):
        rows[pl.ds(tile * ref.shape[0], ref.shape[0]), :] = ref[:, tile * lanes : (tile + 1) * lanes]


def row_tile(rows, row, count, sub):
    return rows[pl.ds(row, sub, stride=count), :]


def mix(taps, now, one, two):
    return [taps[part] * now[part] + taps[3 + part] * one[part] + taps[6 + part] * two[part] for part in range(3)]


def scaled(rows, link):
    return [row * link for row in rows]


def link_at(starts, low, high):
    return jnp.where(hits(starts, low, high), 0.0, 1.0).astype(jnp.float32)


def first_pass(lengths_hbm, x_hbm, taps_hbm, rate_hbm, state_ref, product_ref, query_ref, consts_ref,
               lengths, held, spread, taps_held, rate_held, rate_rows, taps_rows, sems, x_sems):
    toks, sub, lanes = product_ref.shape
    poles = rate_held.shape[0]
    pitch = toks + PAD
    pieces = held.shape[0]
    span = toks // pieces
    small = [
        pltpu.make_async_copy(source, target, sems.at[i])
        for i, (source, target) in enumerate(
            [(lengths_hbm, lengths), (taps_hbm, taps_held), (rate_hbm, rate_held)]
        )
    ]
    for copy in small:
        copy.start()

    def piece_copy(piece):
        return pltpu.make_async_copy(
            x_hbm.at[:, pl.ds(pl.multiple_of(piece * span, span), span), :], held.at[piece], x_sems.at[piece]
        )

    for piece in range(pieces):
        piece_copy(piece).start()
    for copy in small:
        copy.wait()
    anchor = lax.axis_index(CTX) * toks
    starts = starts_of(lengths, anchor)
    as_tiles(rate_rows, rate_held, sub, lanes)
    for tap in range(3):
        for part in range(3):
            for tile in range(sub):
                taps_rows[tap * 3 + part, pl.ds(tile, 1), :] = taps_held[
                    tap, pl.ds(part, 1), tile * lanes : (tile + 1) * lanes
                ]
    fades = []
    for n in range(poles):
        rate = row_tile(rate_rows, n, poles, sub)
        consts_ref[n] = rate
        fades.append(jnp.exp(-rate))
    for row in range(9):
        consts_ref[poles + row] = taps_rows[row]
    state_ref[...] = jnp.zeros_like(state_ref)

    def token_rows(t):
        return [spread[part, pl.ds(t + PAD, sub, stride=pitch), :] for part in range(3)]

    def chunk(index, _):
        base = index * CHUNK

        def steps(masked):
            states = [state_ref[n] for n in range(poles)]
            two, one = token_rows(base - 2), token_rows(base - 1)
            for i in range(CHUNK):
                t = base + i
                now = token_rows(t)
                if masked:
                    link = link_at(starts, t, t + 1)
                    mixed = mix(taps_rows, now, scaled(one, link), scaled(two, link_at(starts, t - 1, t + 1)))
                    states = scaled(states, link)
                else:
                    mixed = mix(taps_rows, now, one, two)
                product = mixed[1] * mixed[2]
                query_ref[t] = mixed[0]
                product_ref[t] = product
                if masked and i < 2:
                    product = jnp.where(index == 0, 0.0, product)
                states = [fades[n] * states[n] + product for n in range(poles)]
                two, one = one, now
            for n in range(poles):
                state_ref[n] = states[n]

        cut = hits(starts, base - 1, base + CHUNK) | (index == 0)

        @pl.when(cut)
        def _():
            steps(True)

        @pl.when(jnp.logical_not(cut))
        def _():
            steps(False)

        return 0

    def piece_step(piece, _):
        piece_copy(piece).wait()
        for part in range(3):
            for tile in range(sub):
                row = pl.multiple_of(piece * span, span) + (tile * pitch + PAD)
                spread[part, pl.ds(pl.multiple_of(row, 8), span), :] = held[
                    piece, part, :, tile * lanes : (tile + 1) * lanes
                ].astype(jnp.float32)
        lax.fori_loop(piece * (span // CHUNK), (piece + 1) * (span // CHUNK), chunk, 0)
        return 0

    lax.fori_loop(0, pieces, piece_step, 0)
    for i in range(2):
        for part, row in enumerate(token_rows(i)):
            consts_ref[poles + 9 + i * 3 + part] = row


def edge_pass(toks, lengths, edge_ref, consts_ref, state_ref, ends_ref, head_ref, spread):
    poles, sub, lanes = state_ref.shape
    anchor = lax.axis_index(CTX) * toks
    starts = starts_of(lengths, anchor)
    for part in range(3):
        for tile in range(sub):
            spread[part, pl.ds(tile * 2, 2), :] = edge_ref[
                part, :, tile * lanes : (tile + 1) * lanes
            ].astype(jnp.float32)
    earlier = [[spread[part, pl.ds(i, sub, stride=2), :] for part in range(3)] for i in range(2)]
    heads = [[consts_ref[poles + 9 + i * 3 + part] for part in range(3)] for i in range(2)]
    taps = [consts_ref[poles + row] for row in range(9)]
    at_zero = mix(taps, heads[0], scaled(earlier[1], link_at(starts, 0, 1)), scaled(earlier[0], link_at(starts, -1, 1)))
    at_one = mix(taps, heads[1], scaled(heads[0], link_at(starts, 1, 2)), scaled(earlier[1], link_at(starts, 0, 2)))
    zero, one = at_zero[1] * at_zero[2], at_one[1] * at_one[2]
    head_ref[0], head_ref[1], head_ref[2], head_ref[3] = zero, one, at_zero[0], at_one[0]
    zero, one = zero * link_at(starts, 1, toks), one * link_at(starts, 2, toks)
    for n in range(poles):
        rate = consts_ref[n]
        late = jnp.exp(rate * (-float(toks - 2)))
        ends_ref[n] = state_ref[n] + late * (jnp.exp(-rate) * zero + one)


def whole(starts, first, count):
    return link_at(starts, first, first + count)


def block_totals(toks, lengths, ends_ref, consts_ref, totals_ref):
    rows, near = lax.axis_size("row"), lax.axis_size("near")
    far = lax.axis_size("far")
    keep = jnp.exp(consts_ref[lax.axis_index("row") * near + lax.axis_index("near")] * (-float(toks)))
    starts = starts_of(lengths, 0)
    for row in range(rows):
        first = (row * far + lax.axis_index("far")) * (near * toks)
        total = ends_ref[row * near]
        for i in range(1, near):
            total = ends_ref[row * near + i] + total * (keep * whole(starts, first + i * toks, toks))
        for g in range(far):
            totals_ref[g * rows + row] = total


def spread_carry(toks, lengths, ends_ref, totals_ref, consts_ref, arrived_ref):
    rows, near, far = lax.axis_size("row"), lax.axis_size("near"), lax.axis_size("far")
    mine = lax.axis_index("far")
    rate = consts_ref[lax.axis_index("row") * near + lax.axis_index("near")]
    span = near * toks
    keep, keep_span = jnp.exp(rate * (-float(toks))), jnp.exp(rate * (-float(span)))
    starts = starts_of(lengths, 0)
    carry = jnp.zeros_like(keep)
    for row in range(rows):
        mid = carry
        for g in range(far):
            mid = jnp.where(g == mine, carry, mid)
            carry = totals_ref[g * rows + row] + carry * (keep_span * whole(starts, (row * far + g) * span, span))
        first = (row * far + mine) * span
        for i in range(near):
            arrived_ref[row * near + i] = mid
            mid = ends_ref[row * near + i] + mid * (keep * whole(starts, first + i * toks, toks))


def second_pass(lengths, arrived_ref, head_ref, product_ref, query_ref, consts_ref, residue_ref, skip_ref,
                response_ref, squares_ref, spread, states_ref, residue_rows):
    toks, sub, lanes = product_ref.shape
    poles = residue_ref.shape[0]
    anchor = lax.axis_index(CTX) * toks
    starts = starts_of(lengths, anchor)
    as_tiles(residue_rows, residue_ref, sub, lanes)
    fades, gains = [], []
    for n in range(poles):
        rate = consts_ref[n]
        fades.append(jnp.exp(-rate))
        gains.append(row_tile(residue_rows, n, poles, sub) * jnp.sqrt(1.0 - jnp.exp(-2.0 * rate)))
    skip = skip_ref[...]
    states_ref[...] = arrived_ref[...]

    def chunk(index, _):
        base = index * CHUNK

        def steps(masked):
            states = [states_ref[n] for n in range(poles)]
            for i in range(CHUNK):
                t = base + i
                product, query = product_ref[t], query_ref[t]
                if masked:
                    states = scaled(states, link_at(starts, t, t + 1))
                    if i < 2:
                        product = jnp.where(index == 0, head_ref[i], product)
                        query = jnp.where(index == 0, head_ref[2 + i], query)
                states = [fades[n] * states[n] + product for n in range(poles)]
                sums = [gains[n] * states[n] for n in range(poles)] + [skip * product]
                while len(sums) > 1:
                    sums = [a + b for a, b in zip(sums[::2], sums[1::2])] + (
                        [sums[-1]] if len(sums) % 2 else []
                    )
                spread[pl.ds(t, sub, stride=toks), :] = query * sums[0]
            for n in range(poles):
                states_ref[n] = states[n]

        cut = hits(starts, base, base + CHUNK) | (index == 0)

        @pl.when(cut)
        def _():
            steps(True)

        @pl.when(jnp.logical_not(cut))
        def _():
            steps(False)

        return 0

    lax.fori_loop(0, toks // CHUNK, chunk, 0)
    total = jnp.zeros((toks, lanes), jnp.float32)
    for tile in range(sub):
        part = spread[pl.ds(tile * toks, toks), :]
        response_ref[:, tile * lanes : (tile + 1) * lanes] = part
        total = total + part * part
    sums = lax.dot_general(
        jnp.ones((squares_ref.shape[0], lanes), jnp.float32), total, (((1,), (1,)), ((), ())),
        precision=HIGH, preferred_element_type=jnp.float32,
    )
    halves = toks // lanes
    half = lax.broadcasted_iota(jnp.int32, squares_ref.shape, 0) % halves
    picked = sums[:, :lanes]
    for h in range(1, halves):
        picked = jnp.where(half == h, sums[:, h * lanes : (h + 1) * lanes], picked)
    squares_ref[...] = picked


def last_pass(squares_ref, response_ref, gain_ref, out_ref):
    count, lanes = squares_ref.shape
    halves = out_ref.shape[0] // lanes
    half = lax.broadcasted_iota(jnp.int32, (count, lanes), 0) % halves
    for h in range(halves):
        sums = lax.dot_general(
            squares_ref[...], (half == h).astype(jnp.float32), (((0,), (0,)), ((), ())),
            precision=HIGH, preferred_element_type=jnp.float32,
        )
        scale = lax.rsqrt(sums / D + eps_norm)
        toks = slice(h * lanes, (h + 1) * lanes)
        for tile in range(response_ref.shape[1] // lanes):
            cols = slice(tile * lanes, (tile + 1) * lanes)
            out_ref[toks, cols] = (response_ref[toks, cols] * scale * gain_ref[:, cols]).astype(jnp.bfloat16)


SCALARS = pl.BlockSpec(memory_space=pltpu.SMEM)
VECTORS = pl.BlockSpec(memory_space=pltpu.VMEM)
ANYWHERE = pl.BlockSpec(memory_space=pltpu.HBM)
F32 = jnp.float32
SPECS = {"s": SCALARS, "v": VECTORS, "a": ANYWHERE}


def call(body, inputs, outputs, scratch, name):
    return pl.pallas_call(
        body,
        in_specs=[SPECS[i] for i in inputs],
        out_specs=jax.tree.map(lambda _: VECTORS, outputs),
        out_shape=outputs,
        scratch_shapes=scratch,
        compiler_params=pltpu.CompilerParams(vmem_limit_bytes=40 << 20),
        name=name,
    )


def shards(features, short_taps, decay_rate, residue, skip_gain, norm_gain, contig_lengths):
    toks, _, channels = features.shape
    poles = decay_rate.shape[0]
    lanes, sub = 128, channels // 128
    count, wide = lax.axis_size(CTX), lax.axis_size("chan")
    tile = lambda *lead: jax.ShapeDtypeStruct((*lead, sub, lanes), F32)
    flat = lambda *dims: jax.ShapeDtypeStruct(dims, F32)
    rows = pltpu.VMEM((poles * sub, lanes), F32)
    parts = jnp.transpose(features, (1, 0, 2))
    edge = lax.ppermute(parts[:, toks - 2 :], CTX, [(i, i + 1) for i in range(count - 1)])
    state, product, query, consts = call(
        first_pass, "aaaa", (tile(poles), tile(toks), tile(toks), tile(poles + 16)),
        [
            pltpu.SMEM(contig_lengths.shape, jnp.int32),
            pltpu.VMEM((PIECES, 3, toks // PIECES, channels), jnp.bfloat16),
            pltpu.VMEM((3, sub * (toks + PAD), lanes), F32),
            pltpu.VMEM(short_taps.shape, F32),
            pltpu.VMEM(decay_rate.shape, F32),
            rows,
            pltpu.VMEM((9, sub, lanes), F32),
            pltpu.SemaphoreType.DMA((3,)),
            pltpu.SemaphoreType.DMA((PIECES,)),
        ],
        "first_pass",
    )(*[pltpu.with_memory_space_constraint(a, pltpu.HBM) for a in (contig_lengths, parts, short_taps, decay_rate)])
    ends, head = call(
        functools.partial(edge_pass, toks), "svvv", (tile(poles), tile(4)),
        [pltpu.VMEM((3, sub * 2, lanes), F32)], "edge_pass",
    )(contig_lengths, edge, consts, state)
    ends = lax.all_to_all(ends, ("row", "near"), 0, 0, tiled=True)
    totals = call(
        functools.partial(block_totals, toks), "svv",
        tile(lax.axis_size("row") * lax.axis_size("far")), [], "block_totals",
    )(contig_lengths, ends, consts)
    totals = lax.all_to_all(totals, "far", 0, 0, tiled=True)
    arrived = call(
        functools.partial(spread_carry, toks), "svvv", tile(poles), [], "spread_carry"
    )(contig_lengths, ends, totals, consts)
    arrived = lax.all_to_all(arrived, ("row", "near"), 0, 0, tiled=True)
    response, squares = call(
        second_pass, "svvvvvvv", (flat(toks, channels), flat(wide * toks // lanes, lanes)),
        [pltpu.VMEM((sub * toks, lanes), F32), pltpu.VMEM((poles, sub, lanes), F32), rows],
        "second_pass",
    )(contig_lengths, arrived, head, product, query, consts, residue,
      jnp.reshape(skip_gain, (sub, lanes)))
    squares = lax.all_to_all(squares, "chan", 0, 0, tiled=True)
    return call(
        last_pass, "vvv", jax.ShapeDtypeStruct((toks, channels), jnp.bfloat16), [], "last_pass"
    )(squares, response, jnp.reshape(norm_gain, (1, channels)))


def solution(mesh):
    chan = mesh.shape["chan"]
    inner = Mesh(mesh.devices.reshape(4, -1, 4, chan), CTX + ("chan",))
    placed = (
        P(CTX, None, "chan"),
        P(None, None, "chan"),
        P(None, "chan"),
        P(None, "chan"),
        P("chan"),
        P("chan"),
        P(),
    )
    return jax.shard_map(
        shards, mesh=inner, in_specs=placed, out_specs=P(CTX, "chan"), check_vma=False
    )
```

time: 120 us -> 108 us (0.900)
  blocking collectives: 101 us -> 91.1 us
  local copies, waits for them, and re-layouts: 4.54 us -> 0.85 us
  Pallas kernels: 8.65 us -> 10.8 us
    all_to_all x2 -> x3, blocking collectives: 88.7 us -> 75.8 us  [the longest x1 41.3 us: shards(): totals = lax.all_to_all(totals, 'far', 0, 0, tiled=True)]
    unnamed x14 -> x8, local copies, waits for them, and re-layouts: 3.71 us -> 0.02 us
    all_to_all x1, blocking collectives: 12.7 us -> 15.3 us  [shards(): squares = lax.all_to_all(squares, 'chan', 0, 0, tiled=True)]
    pallas_call x4 -> x6, Pallas kernels: 8.65 us -> 10.8 us  [the longest x1 3.84 us: shards(): call(first_pass, 'aaaa', (tile(poles), tile(toks), tile(toks), tile(poles...]
  transfers between devices with their start and end apart: 1 -> 1, of which waited for: 1 -> 0; matrix products, arithmetic and copies ran while one was open for 0% -> 0% of each run, Pallas kernels for 0% -> 4%
where the time goes in v2:
time: 108 us; the launch traced here: 107 us
  blocking collectives  91.1 us (84%)
  Pallas kernels  10.8 us (10%)
  starting transfers between devices  4.5 us (4%)
    all_to_all x1, blocking collectives, shards(): totals = lax.all_to_all(totals, 'far', 0, 0, tiled=True)  41.3 us
    all_to_all x1, blocking collectives, shards(): ends = lax.all_to_all(ends, ('row', 'near'), 0, 0, tiled=True)  23.2 us
    all_to_all x1, blocking collectives, shards(): squares = lax.all_to_all(squares, 'chan', 0, 0, tiled=True)  15.3 us
    all_to_all x1, blocking collectives, shards(): arrived = lax.all_to_all(arrived, ('row', 'near'), 0, 0, tiled=True)  11.4 us
    ppermute x1, starting transfers between devices, shards(): lax.ppermute(parts[:, toks - 2:], CTX, [(i, i + 1) for i in range(count -...  4.5 us
    pallas_call x1, Pallas kernels, shards(): call(first_pass, 'aaaa', (tile(poles), tile(toks), tile(toks), tile(poles...  3.84 us
    pallas_call x1, Pallas kernels, shards(): call(second_pass, 'svvvvvvv', (flat(toks, channels), flat(wide * toks //...  3.69 us
  transfers between devices with their start and end apart: 1, of which 0 were waited for; matrix products, arithmetic and copies ran while one was open for 0% of the time, Pallas kernels for 4%

profile of v2, /device:TPU:1, one launch (start us, length us, event | category | flops | bytes accessed | tf_op | source)
XLA Modules:
  0.0 107.3 jit_solution(5928818827202090083)
XLA Ops:
  0.0 0.0 copy-start.1
  0.0 0.8 slice.4
  0.8 0.0 copy-start
  0.8 0.0 copy-start.2
  0.9 4.5 %collective-permute-start = (bf16[3,2,1024]{2,1,0:T(2,128)(2,1)S(1)}, bf16[3,2,1024]{2,1,0:T(2,128)(2,1)S(1)}, u32[]{:S(2)}, u32[]{:S(2)}) collective-permute-start(bf16[3,2,1024]{2,1,0:T(2,128)(2,1)S(1)} %slice.4), channel_id=1, source_target_pairs={{0,8},{8,16},{16,24},{24,32},{32,40},{40,48},{48,56},{56,64},{64,7... | collective-permute-start | bytes 36872 | tf_op jit(solution)/shard_map/ppermute | solution.py:326
  5.4 3.8 %first_pass.1 = (f32[16,8,128]{2,1,0:T(8,128)S(1)}, f32[256,8,128]{2,1,0:T(8,128)S(1)}, f32[256,8,128]{2,1,0:T(8,128)S(1)}, f32[32,8,128]{2,1,0:T(8,128)S(1)}) custom-call(s32[4]{0:T(128)} %lengths.7, bf16[3,256,1024]{2,1,0:T(8,128)(2,1)} %bitcast.10, f32[3,3,1024]{2,1,0:T(4,128)} %taps_hbm.1, f32[16,1024]{1,0:T(8,128)} %rate_hbm.1), custom_call_target="tpu_custom_call" | custom-call | tf_op jit(solution)/shard_map/first_pass/pallas_call | solution.py:327
  9.2 0.0 collective-permute-done.edge_ref
  9.2 0.0 copy-done.1
  9.2 0.6 edge_pass.1
  9.9 23.2 %all_to_all.26.ends_ref = f32[16,8,128]{2,1,0:T(8,128)S(1)} all-to-all(f32[16,8,128]{2,1,0:T(8,128)S(1)} %get-tuple-element.15), channel_id=1, replica_groups=mesh['row'=4,'far'=8,'near'=4,'chan'=8] {'row','near'}, dimensions={0} | all-to-all | bytes 131072 | tf_op jit(solution)/shard_map/all_to_all | solution.py:346
  33.0 0.6 block_totals.1
  33.7 0.0 copy-start.3
  33.7 41.3 %all_to_all.27.totals_ref = f32[32,8,128]{2,1,0:T(8,128)S(1)} all-to-all(f32[32,8,128]{2,1,0:T(8,128)S(1)} %block_totals.1), channel_id=1, replica_groups=mesh['row'=4,'far'=8,'near'=4,'chan'=8] {'far'}, dimensions={0} | all-to-all | bytes 262144 | tf_op jit(solution)/shard_map/all_to_all | solution.py:351
  75.0 0.8 spread_carry.1
  75.7 11.4 %all_to_all.28.arrived_ref = f32[16,8,128]{2,1,0:T(8,128)S(1)} all-to-all(f32[16,8,128]{2,1,0:T(8,128)S(1)} %spread_carry.1), channel_id=1, replica_groups=mesh['row'=4,'far'=8,'near'=4,'chan'=8] {'row','near'}, dimensions={0} | all-to-all | bytes 131072 | tf_op jit(solution)/shard_map/all_to_all | solution.py:355
  87.1 0.0 copy-done
  87.1 0.0 copy-done.2
  87.1 3.7 %second_pass.1 = (f32[256,1024]{1,0:T(8,128)S(1)}, f32[16,128]{1,0:T(8,128)S(1)}) custom-call(s32[4]{0:T(128)S(1)} %copy-done.1, f32[16,8,128]{2,1,0:T(8,128)S(1)} %all_to_all.28.arrived_ref, f32[4,8,128]{2,1,0:T(8,128)S(1)} %get-tuple-element.16.head_ref, f32[256,8,128]{2,1,0:T(8,128)S(1)} %get-tuple-element.17.product_ref, ...), custom_call_target="tpu_custom_call" | custom-call | tf_op jit(solution)/shard_map/second_pass/pallas_call | solution.py:356
  90.8 15.3 %all_to_all.29 = f32[8,2,128]{2,1,0:T(2,128)S(1)} all-to-all(f32[8,2,128]{2,1,0:T(2,128)S(1)} %bitcast.6), channel_id=1, replica_groups=mesh['row'=4,'far'=8,'near'=4,'chan'=8] {'chan'}, dimensions={0} | all-to-all | bytes 16384 | tf_op jit(solution)/shard_map/all_to_all | solution.py:362
  106.1 0.0 copy-done.3
  106.1 1.2 %last_pass.1 = bf16[256,1024]{1,0:T(8,128)(2,1)} custom-call(f32[16,128]{1,0:T(8,128)S(1)} %bitcast.5, f32[256,1024]{1,0:T(8,128)S(1)} %get-tuple-element.20.response_ref, f32[1,1024]{1,0:T(1,128)S(1)} %bitcast.8), custom_call_target="tpu_custom_call" | custom-call | tf_op jit(solution)/shard_map/last_pass/pallas_call | solution.py:363
Async XLA Ops:
  0.0 9.2 %copy-start.1 = (s32[4]{0:T(128)S(1)}, s32[4]{0:T(128)}, u32[]{:S(2)}) copy-start(s32[4]{0:T(128)} %lengths.7) | copy-start | bytes 52
  0.8 86.3 %copy-start = (f32[16,1024]{1,0:T(8,128)S(1)}, f32[16,1024]{1,0:T(8,128)}, u32[]{:S(2)}) copy-start(f32[16,1024]{1,0:T(8,128)} %residue_ref.1) | copy-start | bytes 196612
  0.8 86.3 %copy-start.2 = (f32[1024]{0:T(1024)S(1)}, f32[1024]{0:T(1024)}, u32[]{:S(2)}) copy-start(f32[1024]{0:T(1024)} %param.11) | copy-start | bytes 12292
  0.9 8.4 %collective-permute-start = (bf16[3,2,1024]{2,1,0:T(2,128)(2,1)S(1)}, bf16[3,2,1024]{2,1,0:T(2,128)(2,1)S(1)}, u32[]{:S(2)}, u32[]{:S(2)}) collective-permute-start(bf16[3,2,1024]{2,1,0:T(2,128)(2,1)S(1)} %slice.4), channel_id=1, source_target_pairs={{0,8},{8,16},{16,24},{24,32},{32,40},{40,48},{48,56},{56,64},{64,7... | collective-permute-start | bytes 36872 | tf_op jit(solution)/shard_map/ppermute | solution.py:326
  33.7 72.4 %copy-start.3 = (f32[1024]{0:T(1024)S(1)}, f32[1024]{0:T(1024)}, u32[]{:S(2)}) copy-start(f32[1024]{0:T(1024)} %param.12) | copy-start | bytes 12292

commit v3 on v2

--- a/solution.py
+++ b/solution.py
@@ -9,9 +9,9 @@
 
 D = 8192
 eps_norm = 1e-05
-CHUNK = 16
+CHUNK = 32
 PAD = 8
-PIECES = 4
+PIECES = 2
 CTX = ("row", "far", "near")
 HIGH = lax.Precision.HIGHEST
 
@@ -37,6 +37,10 @@
 
 def row_tile(rows, row, count, sub):
     return rows[pl.ds(row, sub, stride=count), :]
+
+
+def is_early():
+    return lax.axis_index("far") < lax.axis_size("far") // 4
 
 
 def mix(taps, now, one, two):
@@ -151,7 +155,9 @@
             consts_ref[poles + 9 + i * 3 + part] = row
 
 
-def edge_pass(toks, lengths, edge_ref, consts_ref, state_ref, ends_ref, head_ref, spread):
+def edge_pass(lengths, edge_ref, consts_ref, state_ref, product_ref, residue_ref, skip_ref,
+              ends_ref, head_ref, local_ref, gains_ref, spread, states_ref, residue_rows):
+    toks = product_ref.shape[0]
     poles, sub, lanes = state_ref.shape
     anchor = lax.axis_index(CTX) * toks
     starts = starts_of(lengths, anchor)
@@ -173,6 +179,18 @@
         late = jnp.exp(rate * (-float(toks - 2)))
         ends_ref[n] = state_ref[n] + late * (jnp.exp(-rate) * zero + one)
 
+    @pl.when(is_early())
+    def _():
+        fades, gains = fades_and_gains(consts_ref, residue_ref, residue_rows, sub, lanes)
+        for n in range(poles):
+            gains_ref[n] = gains[n]
+        states_ref[...] = jnp.zeros_like(states_ref)
+
+        def emit(t, _, product, total):
+            local_ref[t] = total
+
+        recurrence(starts, fades, gains, skip_ref[...], head_ref, product_ref, None, states_ref, emit)
+
 
 def whole(starts, first, count):
     return link_at(starts, first, first + count)
@@ -211,20 +229,26 @@
             mid = ends_ref[row * near + i] + mid * (keep * whole(starts, first + i * toks, toks))
 
 
-def second_pass(lengths, arrived_ref, head_ref, product_ref, query_ref, consts_ref, residue_ref, skip_ref,
-                response_ref, squares_ref, spread, states_ref, residue_rows):
-    toks, sub, lanes = product_ref.shape
-    poles = residue_ref.shape[0]
-    anchor = lax.axis_index(CTX) * toks
-    starts = starts_of(lengths, anchor)
+def fades_and_gains(consts_ref, residue_ref, residue_rows, sub, lanes):
     as_tiles(residue_rows, residue_ref, sub, lanes)
     fades, gains = [], []
-    for n in range(poles):
+    for n in range(residue_ref.shape[0]):
         rate = consts_ref[n]
         fades.append(jnp.exp(-rate))
-        gains.append(row_tile(residue_rows, n, poles, sub) * jnp.sqrt(1.0 - jnp.exp(-2.0 * rate)))
-    skip = skip_ref[...]
-    states_ref[...] = arrived_ref[...]
+        gains.append(
+            row_tile(residue_rows, n, residue_ref.shape[0], sub) * jnp.sqrt(1.0 - jnp.exp(-2.0 * rate))
+        )
+    return fades, gains
+
+
+def summed(terms):
+    while len(terms) > 1:
+        terms = [a + b for a, b in zip(terms[::2], terms[1::2])] + ([terms[-1]] if len(terms) % 2 else [])
+    return terms[0]
+
+
+def recurrence(starts, fades, gains, skip, head_ref, product_ref, query_ref, states_ref, emit):
+    poles = len(fades)
 
     def chunk(index, _):
         base = index * CHUNK
@@ -233,19 +257,16 @@
             states = [states_ref[n] for n in range(poles)]
             for i in range(CHUNK):
                 t = base + i
-                product, query = product_ref[t], query_ref[t]
+                product = product_ref[t]
+                query = None if query_ref is None else query_ref[t]
                 if masked:
                     states = scaled(states, link_at(starts, t, t + 1))
                     if i < 2:
                         product = jnp.where(index == 0, head_ref[i], product)
-                        query = jnp.where(index == 0, head_ref[2 + i], query)
+                        if query is not None:
+                            query = jnp.where(index == 0, head_ref[2 + i], query)
                 states = [fades[n] * states[n] + product for n in range(poles)]
-                sums = [gains[n] * states[n] for n in range(poles)] + [skip * product]
-                while len(sums) > 1:
-                    sums = [a + b for a, b in zip(sums[::2], sums[1::2])] + (
-                        [sums[-1]] if len(sums) % 2 else []
-                    )
-                spread[pl.ds(t, sub, stride=toks), :] = query * sums[0]
+                emit(t, query, product, summed([gains[n] * states[n] for n in range(poles)] + [skip * product]))
             for n in range(poles):
                 states_ref[n] = states[n]
 
@@ -261,7 +282,63 @@
 
         return 0
 
-    lax.fori_loop(0, toks // CHUNK, chunk, 0)
+    lax.fori_loop(0, product_ref.shape[0] // CHUNK, chunk, 0)
+
+
+def second_pass(lengths, arrived_ref, head_ref, local_ref, gains_ref, product_ref, query_ref, consts_ref,
+                residue_ref, skip_ref, response_ref, squares_ref, spread, states_ref, residue_rows):
+    toks, sub, lanes = product_ref.shape
+    poles = residue_ref.shape[0]
+    starts = starts_of(lengths, lax.axis_index(CTX) * toks)
+
+    @pl.when(is_early())
+    def _():
+        fades = [jnp.exp(-consts_ref[n]) for n in range(poles)]
+        for n in range(poles):
+            states_ref[n] = arrived_ref[n] * gains_ref[n]
+
+        def chunk(index, _):
+            base = index * CHUNK
+
+            def steps(masked):
+                states = [states_ref[n] for n in range(poles)]
+                for i in range(CHUNK):
+                    t = base + i
+                    query = query_ref[t]
+                    states = [fades[n] * states[n] for n in range(poles)]
+                    incoming = summed(list(states))
+                    if masked:
+                        incoming = incoming * link_at(starts, 0, t + 1)
+                        if i < 2:
+                            query = jnp.where(index == 0, head_ref[2 + i], query)
+                    spread[pl.ds(t, sub, stride=toks), :] = query * (local_ref[t] + incoming)
+                for n in range(poles):
+                    states_ref[n] = states[n]
+
+            cut = hits(starts, 0, base + CHUNK) | (index == 0)
+
+            @pl.when(cut)
+            def _():
+                steps(True)
+
+            @pl.when(jnp.logical_not(cut))
+            def _():
+                steps(False)
+
+            return 0
+
+        lax.fori_loop(0, toks // CHUNK, chunk, 0)
+
+    @pl.when(jnp.logical_not(is_early()))
+    def _():
+        fades, gains = fades_and_gains(consts_ref, residue_ref, residue_rows, sub, lanes)
+        states_ref[...] = arrived_ref[...]
+
+        def emit(t, query, _, total):
+            spread[pl.ds(t, sub, stride=toks), :] = query * total
+
+        recurrence(starts, fades, gains, skip_ref[...], head_ref, product_ref, query_ref, states_ref, emit)
+
     total = jnp.zeros((toks, lanes), jnp.float32)
     for tile in range(sub):
         part = spread[pl.ds(tile * toks, toks), :]
@@ -339,10 +416,12 @@
         ],
         "first_pass",
     )(*[pltpu.with_memory_space_constraint(a, pltpu.HBM) for a in (contig_lengths, parts, short_taps, decay_rate)])
-    ends, head = call(
-        functools.partial(edge_pass, toks), "svvv", (tile(poles), tile(4)),
-        [pltpu.VMEM((3, sub * 2, lanes), F32)], "edge_pass",
-    )(contig_lengths, edge, consts, state)
+    states = pltpu.VMEM((poles, sub, lanes), F32)
+    skip = jnp.reshape(skip_gain, (sub, lanes))
+    ends, head, local, gains = call(
+        edge_pass, "svvvvvv", (tile(poles), tile(4), tile(toks), tile(poles)),
+        [pltpu.VMEM((3, sub * 2, lanes), F32), states, rows], "edge_pass",
+    )(contig_lengths, edge, consts, state, product, residue, skip)
     ends = lax.all_to_all(ends, ("row", "near"), 0, 0, tiled=True)
     totals = call(
         functools.partial(block_totals, toks), "svv",
@@ -354,11 +433,9 @@
     )(contig_lengths, ends, totals, consts)
     arrived = lax.all_to_all(arrived, ("row", "near"), 0, 0, tiled=True)
     response, squares = call(
-        second_pass, "svvvvvvv", (flat(toks, channels), flat(wide * toks // lanes, lanes)),
-        [pltpu.VMEM((sub * toks, lanes), F32), pltpu.VMEM((poles, sub, lanes), F32), rows],
-        "second_pass",
-    )(contig_lengths, arrived, head, product, query, consts, residue,
-      jnp.reshape(skip_gain, (sub, lanes)))
+        second_pass, "svvvvvvvvv", (flat(toks, channels), flat(wide * toks // lanes, lanes)),
+        [pltpu.VMEM((sub * toks, lanes), F32), states, rows], "second_pass",
+    )(contig_lengths, arrived, head, local, gains, product, query, consts, residue, skip)
     squares = lax.all_to_all(squares, "chan", 0, 0, tiled=True)
     return call(
         last_pass, "vvv", jax.ShapeDtypeStruct((toks, channels), jnp.bfloat16), [], "last_pass"

time: 108 us -> 106 us (0.981)
  blocking collectives: 91.1 us -> 88.6 us
  Pallas kernels: 10.8 us -> 12 us
    all_to_all x1, blocking collectives: 41.3 us -> 38.6 us  [shards(): totals = lax.all_to_all(totals, 'far', 0, 0, tiled=True)]
    pallas_call x2, Pallas kernels: 4.3 us -> 5.75 us  [the longest x1 3.11 us: shards(): call(edge_pass, 'svvvvvv', (tile(poles), tile(4), tile(toks), tile(poles)...]
  transfers between devices with their start and end apart: 1 -> 1, of which waited for: 0 -> 0; matrix products, arithmetic and copies ran while one was open for 0% -> 0% of each run, Pallas kernels for 4% -> 3%
where the time goes in v3:
time: 106 us
  blocking collectives  88.6 us (84%)
  Pallas kernels  12 us (11%)
  starting transfers between devices  4.37 us (4%)
    all_to_all x1, blocking collectives, shards(): totals = lax.all_to_all(totals, 'far', 0, 0, tiled=True)  38.6 us
    all_to_all x1, blocking collectives, shards(): ends = lax.all_to_all(ends, ('row', 'near'), 0, 0, tiled=True)  23.4 us
    all_to_all x1, blocking collectives, shards(): squares = lax.all_to_all(squares, 'chan', 0, 0, tiled=True)  15.3 us
    all_to_all x1, blocking collectives, shards(): arrived = lax.all_to_all(arrived, ('row', 'near'), 0, 0, tiled=True)  11.4 us
    ppermute x1, starting transfers between devices, shards(): lax.ppermute(parts[:, toks - 2:], CTX, [(i, i + 1) for i in range(count -...  4.37 us
    pallas_call x1, Pallas kernels, shards(): call(first_pass, 'aaaa', (tile(poles), tile(toks), tile(toks), tile(poles...  3.64 us
    pallas_call x1, Pallas kernels, shards(): call(edge_pass, 'svvvvvv', (tile(poles), tile(4), tile(toks), tile(poles)...  3.11 us
    pallas_call x1, Pallas kernels, shards(): call(second_pass, 'svvvvvvvvv', (flat(toks, channels), flat(wide * toks /...  2.64 us
  transfers between devices with their start and end apart: 1, of which 0 were waited for; matrix products, arithmetic and copies ran while one was open for 0% of the time, Pallas kernels for 3%

profile of v3, /device:TPU:1, one launch (start us, length us, event | category | flops | bytes accessed | tf_op | source)
XLA Modules:
  0.0 105.9 jit_solution(15884765955845545635)
XLA Ops:
  0.0 0.0 copy-start.2
  0.0 0.0 copy-start
  0.0 0.0 copy-start.1
  0.0 0.8 slice.4
  0.9 4.4 %collective-permute-start = (bf16[3,2,1024]{2,1,0:T(2,128)(2,1)S(1)}, bf16[3,2,1024]{2,1,0:T(2,128)(2,1)S(1)}, u32[]{:S(2)}, u32[]{:S(2)}) collective-permute-start(bf16[3,2,1024]{2,1,0:T(2,128)(2,1)S(1)} %slice.4), channel_id=1, source_target_pairs={{0,8},{8,16},{16,24},{24,32},{32,40},{40,48},{48,56},{56,64},{64,7... | collective-permute-start | bytes 36872 | tf_op jit(solution)/shard_map/ppermute | solution.py:403
  5.2 3.6 %first_pass.1 = (f32[16,8,128]{2,1,0:T(8,128)S(1)}, f32[256,8,128]{2,1,0:T(8,128)S(1)}, f32[256,8,128]{2,1,0:T(8,128)S(1)}, f32[32,8,128]{2,1,0:T(8,128)S(1)}) custom-call(s32[4]{0:T(128)} %lengths.7, bf16[3,256,1024]{2,1,0:T(8,128)(2,1)} %bitcast.11, f32[3,3,1024]{2,1,0:T(4,128)} %taps_hbm.1, f32[16,1024]{1,0:T(8,128)} %rate_hbm.1), custom_call_target="tpu_custom_call" | custom-call | tf_op jit(solution)/shard_map/first_pass/pallas_call | solution.py:404
  8.9 0.0 collective-permute-done.edge_ref
  8.9 0.0 copy-done.2
  8.9 0.0 copy-done
  8.9 0.0 copy-done.1
  8.9 3.1 %edge_pass.1 = (f32[16,8,128]{2,1,0:T(8,128)S(1)}, f32[4,8,128]{2,1,0:T(8,128)S(1)}, f32[256,8,128]{2,1,0:T(8,128)S(1)}, f32[16,8,128]{2,1,0:T(8,128)S(1)}) custom-call(s32[4]{0:T(128)S(1)} %copy-done.2, bf16[3,2,1024]{2,1,0:T(2,128)(2,1)S(1)} %collective-permute-done.edge_ref, f32[32,8,128]{2,1,0:T(8,128)S(1)} %get-tuple-element.15.consts_ref, ...), custom_call_target="tpu_custom_call" | custom-call | tf_op jit(solution)/shard_map/edge_pass/pallas_call | solution.py:421
  12.1 23.4 %all_to_all.26.ends_ref = f32[16,8,128]{2,1,0:T(8,128)S(1)} all-to-all(f32[16,8,128]{2,1,0:T(8,128)S(1)} %get-tuple-element.18), channel_id=1, replica_groups=mesh['row'=4,'far'=8,'near'=4,'chan'=8] {'row','near'}, dimensions={0} | all-to-all | bytes 131072 | tf_op jit(solution)/shard_map/all_to_all | solution.py:425
  35.4 0.6 block_totals.1
  36.0 38.6 %all_to_all.27.totals_ref = f32[32,8,128]{2,1,0:T(8,128)S(1)} all-to-all(f32[32,8,128]{2,1,0:T(8,128)S(1)} %block_totals.1), channel_id=1, replica_groups=mesh['row'=4,'far'=8,'near'=4,'chan'=8] {'far'}, dimensions={0} | all-to-all | bytes 262144 | tf_op jit(solution)/shard_map/all_to_all | solution.py:430
  74.6 0.8 spread_carry.1
  75.4 11.4 %all_to_all.28.arrived_ref = f32[16,8,128]{2,1,0:T(8,128)S(1)} all-to-all(f32[16,8,128]{2,1,0:T(8,128)S(1)} %spread_carry.1), channel_id=1, replica_groups=mesh['row'=4,'far'=8,'near'=4,'chan'=8] {'row','near'}, dimensions={0} | all-to-all | bytes 131072 | tf_op jit(solution)/shard_map/all_to_all | solution.py:434
  86.8 0.0 copy-start.3
  86.8 2.6 %second_pass.1 = (f32[256,1024]{1,0:T(8,128)S(1)}, f32[16,128]{1,0:T(8,128)S(1)}) custom-call(s32[4]{0:T(128)S(1)} %copy-done.2, f32[16,8,128]{2,1,0:T(8,128)S(1)} %all_to_all.28.arrived_ref, f32[4,8,128]{2,1,0:T(8,128)S(1)} %get-tuple-element.19.head_ref, f32[256,8,128]{2,1,0:T(8,128)S(1)} %get-tuple-element.20.local_ref, ...), custom_call_target="tpu_custom_call" | custom-call | tf_op jit(solution)/shard_map/second_pass/pallas_call | solution.py:435
  89.4 15.3 %all_to_all.29 = f32[8,2,128]{2,1,0:T(2,128)S(1)} all-to-all(f32[8,2,128]{2,1,0:T(2,128)S(1)} %bitcast.8), channel_id=1, replica_groups=mesh['row'=4,'far'=8,'near'=4,'chan'=8] {'chan'}, dimensions={0} | all-to-all | bytes 16384 | tf_op jit(solution)/shard_map/all_to_all | solution.py:439
  104.7 0.0 copy-done.3
  104.7 1.2 %last_pass.1 = bf16[256,1024]{1,0:T(8,128)(2,1)} custom-call(f32[16,128]{1,0:T(8,128)S(1)} %bitcast.5, f32[256,1024]{1,0:T(8,128)S(1)} %get-tuple-element.24.response_ref, f32[1,1024]{1,0:T(1,128)S(1)} %bitcast.9), custom_call_target="tpu_custom_call" | custom-call | tf_op jit(solution)/shard_map/last_pass/pallas_call | solution.py:440
Async XLA Ops:
  0.0 8.9 %copy-start.2 = (s32[4]{0:T(128)S(1)}, s32[4]{0:T(128)}, u32[]{:S(2)}) copy-start(s32[4]{0:T(128)} %lengths.7) | copy-start | bytes 52
  0.0 8.9 %copy-start = (f32[16,1024]{1,0:T(8,128)S(1)}, f32[16,1024]{1,0:T(8,128)}, u32[]{:S(2)}) copy-start(f32[16,1024]{1,0:T(8,128)} %residue_ref.3) | copy-start | bytes 196612
  0.0 8.9 %copy-start.1 = (f32[1024]{0:T(1024)S(1)}, f32[1024]{0:T(1024)}, u32[]{:S(2)}) copy-start(f32[1024]{0:T(1024)} %param.11) | copy-start | bytes 12292
  0.9 8.0 %collective-permute-start = (bf16[3,2,1024]{2,1,0:T(2,128)(2,1)S(1)}, bf16[3,2,1024]{2,1,0:T(2,128)(2,1)S(1)}, u32[]{:S(2)}, u32[]{:S(2)}) collective-permute-start(bf16[3,2,1024]{2,1,0:T(2,128)(2,1)S(1)} %slice.4), channel_id=1, source_target_pairs={{0,8},{8,16},{16,24},{24,32},{32,40},{40,48},{48,56},{56,64},{64,7... | collective-permute-start | bytes 36872 | tf_op jit(solution)/shard_map/ppermute | solution.py:403
  86.8 17.9 %copy-start.3 = (f32[1024]{0:T(1024)S(1)}, f32[1024]{0:T(1024)}, u32[]{:S(2)}) copy-start(f32[1024]{0:T(1024)} %param.12) | copy-start | bytes 12292

commit v4 on v3

--- a/solution.py
+++ b/solution.py
@@ -30,6 +30,16 @@
     return found
 
 
+def marked(marks_ref, anchor):
+    return [marks_ref[k] - anchor for k in range(marks_ref.shape[0])]
+
+
+def marked_scalars(marks_ref, anchor):
+    return [
+        jnp.max(marks_ref[k].astype(jnp.float32)).astype(jnp.int32) - anchor for k in range(marks_ref.shape[0])
+    ]
+
+
 def as_tiles(rows, ref, sub, lanes):
     for tile in range(sub):
         rows[pl.ds(tile * ref.shape[0], ref.shape[0]), :] = ref[:, tile * lanes : (tile + 1) * lanes]
@@ -55,7 +65,7 @@
     return jnp.where(hits(starts, low, high), 0.0, 1.0).astype(jnp.float32)
 
 
-def first_pass(lengths_hbm, x_hbm, taps_hbm, rate_hbm, state_ref, product_ref, query_ref, consts_ref,
+def first_pass(lengths_hbm, x_hbm, taps_hbm, rate_hbm, state_ref, product_ref, query_ref, consts_ref, marks_ref,
                lengths, held, spread, taps_held, rate_held, rate_rows, taps_rows, sems, x_sems):
     toks, sub, lanes = product_ref.shape
     poles = rate_held.shape[0]
@@ -82,6 +92,8 @@
         copy.wait()
     anchor = lax.axis_index(CTX) * toks
     starts = starts_of(lengths, anchor)
+    for k, start in enumerate(starts_of(lengths, 0)):
+        marks_ref[k] = jnp.full((sub, lanes), start, jnp.int32)
     as_tiles(rate_rows, rate_held, sub, lanes)
     for tap in range(3):
         for part in range(3):
@@ -155,12 +167,12 @@
             consts_ref[poles + 9 + i * 3 + part] = row
 
 
-def edge_pass(lengths, edge_ref, consts_ref, state_ref, product_ref, residue_ref, skip_ref,
+def edge_pass(marks_ref, edge_ref, consts_ref, state_ref, product_ref, residue_ref, skip_ref,
               ends_ref, head_ref, local_ref, gains_ref, spread, states_ref, residue_rows):
     toks = product_ref.shape[0]
     poles, sub, lanes = state_ref.shape
     anchor = lax.axis_index(CTX) * toks
-    starts = starts_of(lengths, anchor)
+    starts = marked(marks_ref, anchor)
     for part in range(3):
         for tile in range(sub):
             spread[part, pl.ds(tile * 2, 2), :] = edge_ref[
@@ -189,18 +201,18 @@
         def emit(t, _, product, total):
             local_ref[t] = total
 
-        recurrence(starts, fades, gains, skip_ref[...], head_ref, product_ref, None, states_ref, emit)
+        recurrence(marked_scalars(marks_ref, anchor), fades, gains, skip_ref[...], head_ref, product_ref, None, states_ref, emit)
 
 
 def whole(starts, first, count):
     return link_at(starts, first, first + count)
 
 
-def block_totals(toks, lengths, ends_ref, consts_ref, totals_ref):
+def block_totals(toks, marks_ref, ends_ref, consts_ref, totals_ref):
     rows, near = lax.axis_size("row"), lax.axis_size("near")
     far = lax.axis_size("far")
     keep = jnp.exp(consts_ref[lax.axis_index("row") * near + lax.axis_index("near")] * (-float(toks)))
-    starts = starts_of(lengths, 0)
+    starts = marked(marks_ref, 0)
     for row in range(rows):
         first = (row * far + lax.axis_index("far")) * (near * toks)
         total = ends_ref[row * near]
@@ -210,13 +222,13 @@
             totals_ref[g * rows + row] = total
 
 
-def spread_carry(toks, lengths, ends_ref, totals_ref, consts_ref, arrived_ref):
+def spread_carry(toks, marks_ref, ends_ref, totals_ref, consts_ref, arrived_ref):
     rows, near, far = lax.axis_size("row"), lax.axis_size("near"), lax.axis_size("far")
     mine = lax.axis_index("far")
     rate = consts_ref[lax.axis_index("row") * near + lax.axis_index("near")]
     span = near * toks
     keep, keep_span = jnp.exp(rate * (-float(toks))), jnp.exp(rate * (-float(span)))
-    starts = starts_of(lengths, 0)
+    starts = marked(marks_ref, 0)
     carry = jnp.zeros_like(keep)
     for row in range(rows):
         mid = carry
@@ -285,11 +297,11 @@
     lax.fori_loop(0, product_ref.shape[0] // CHUNK, chunk, 0)
 
 
-def second_pass(lengths, arrived_ref, head_ref, local_ref, gains_ref, product_ref, query_ref, consts_ref,
+def second_pass(marks_ref, arrived_ref, head_ref, local_ref, gains_ref, product_ref, query_ref, consts_ref,
                 residue_ref, skip_ref, response_ref, squares_ref, spread, states_ref, residue_rows):
     toks, sub, lanes = product_ref.shape
     poles = residue_ref.shape[0]
-    starts = starts_of(lengths, lax.axis_index(CTX) * toks)
+    starts = marked_scalars(marks_ref, lax.axis_index(CTX) * toks)
 
     @pl.when(is_early())
     def _():
@@ -401,8 +413,9 @@
     rows = pltpu.VMEM((poles * sub, lanes), F32)
     parts = jnp.transpose(features, (1, 0, 2))
     edge = lax.ppermute(parts[:, toks - 2 :], CTX, [(i, i + 1) for i in range(count - 1)])
-    state, product, query, consts = call(
-        first_pass, "aaaa", (tile(poles), tile(toks), tile(toks), tile(poles + 16)),
+    marks_shape = jax.ShapeDtypeStruct((contig_lengths.shape[0], sub, lanes), jnp.int32)
+    state, product, query, consts, marks = call(
+        first_pass, "aaaa", (tile(poles), tile(toks), tile(toks), tile(poles + 16), marks_shape),
         [
             pltpu.SMEM(contig_lengths.shape, jnp.int32),
             pltpu.VMEM((PIECES, 3, toks // PIECES, channels), jnp.bfloat16),
@@ -419,23 +432,23 @@
     states = pltpu.VMEM((poles, sub, lanes), F32)
     skip = jnp.reshape(skip_gain, (sub, lanes))
     ends, head, local, gains = call(
-        edge_pass, "svvvvvv", (tile(poles), tile(4), tile(toks), tile(poles)),
+        edge_pass, "vvvvvvv", (tile(poles), tile(4), tile(toks), tile(poles)),
         [pltpu.VMEM((3, sub * 2, lanes), F32), states, rows], "edge_pass",
-    )(contig_lengths, edge, consts, state, product, residue, skip)
+    )(marks, edge, consts, state, product, residue, skip)
     ends = lax.all_to_all(ends, ("row", "near"), 0, 0, tiled=True)
     totals = call(
-        functools.partial(block_totals, toks), "svv",
+        functools.partial(block_totals, toks), "vvv",
         tile(lax.axis_size("row") * lax.axis_size("far")), [], "block_totals",
-    )(contig_lengths, ends, consts)
+    )(marks, ends, consts)
     totals = lax.all_to_all(totals, "far", 0, 0, tiled=True)
     arrived = call(
-        functools.partial(spread_carry, toks), "svvv", tile(poles), [], "spread_carry"
-    )(contig_lengths, ends, totals, consts)
+        functools.partial(spread_carry, toks), "vvvv", tile(poles), [], "spread_carry"
+    )(marks, ends, totals, consts)
     arrived = lax.all_to_all(arrived, ("row", "near"), 0, 0, tiled=True)
     response, squares = call(
-        second_pass, "svvvvvvvvv", (flat(toks, channels), flat(wide * toks // lanes, lanes)),
+        second_pass, "vvvvvvvvvv", (flat(toks, channels), flat(wide * toks // lanes, lanes)),
         [pltpu.VMEM((sub * toks, lanes), F32), states, rows], "second_pass",
-    )(contig_lengths, arrived, head, local, gains, product, query, consts, residue, skip)
+    )(marks, arrived, head, local, gains, product, query, consts, residue, skip)
     squares = lax.all_to_all(squares, "chan", 0, 0, tiled=True)
     return call(
         last_pass, "vvv", jax.ShapeDtypeStruct((toks, channels), jnp.bfloat16), [], "last_pass"

time: 106 us -> 104 us (0.981)
  Pallas kernels: 12 us -> 9.89 us
    pallas_call x4, Pallas kernels: 7.15 us -> 5.02 us  [the longest x1 2.65 us: shards(): call(edge_pass, 'vvvvvvv', (tile(poles), tile(4), tile(toks), tile(poles)...]
  transfers between devices with their start and end apart: 1 -> 1, of which waited for: 0 -> 0; matrix products, arithmetic and copies ran while one was open for 0% -> 0% of each run, Pallas kernels for 3% -> 4%
where the time goes in v4:
time: 104 us
  blocking collectives  88.6 us (85%)
  Pallas kernels  9.89 us (10%)
  starting transfers between devices  4.37 us (4%)
    all_to_all x1, blocking collectives, shards(): totals = lax.all_to_all(totals, 'far', 0, 0, tiled=True)  38.6 us
    all_to_all x1, blocking collectives, shards(): ends = lax.all_to_all(ends, ('row', 'near'), 0, 0, tiled=True)  23.3 us
    all_to_all x1, blocking collectives, shards(): squares = lax.all_to_all(squares, 'chan', 0, 0, tiled=True)  15.3 us
    all_to_all x1, blocking collectives, shards(): arrived = lax.all_to_all(arrived, ('row', 'near'), 0, 0, tiled=True)  11.4 us
    ppermute x1, starting transfers between devices, shards(): lax.ppermute(parts[:, toks - 2:], CTX, [(i, i + 1) for i in range(count -...  4.37 us
    pallas_call x1, Pallas kernels, shards(): call(first_pass, 'aaaa', (tile(poles), tile(toks), tile(toks), tile(poles...  3.65 us
    pallas_call x1, Pallas kernels, shards(): call(edge_pass, 'vvvvvvv', (tile(poles), tile(4), tile(toks), tile(poles)...  2.65 us
    pallas_call x1, Pallas kernels, shards(): call(second_pass, 'vvvvvvvvvv', (flat(toks, channels), flat(wide * toks /...  2.14 us
  transfers between devices with their start and end apart: 1, of which 0 were waited for; matrix products, arithmetic and copies ran while one was open for 0% of the time, Pallas kernels for 4%

profile of v4, /device:TPU:1, one launch (start us, length us, event | category | flops | bytes accessed | tf_op | source)
XLA Modules:
  0.0 103.7 jit_solution(4254014476324233577)
XLA Ops:
  0.0 0.0 copy-start
  0.0 0.0 copy-start.1
  0.0 0.8 slice.4
  0.9 4.4 %collective-permute-start = (bf16[3,2,1024]{2,1,0:T(2,128)(2,1)S(1)}, bf16[3,2,1024]{2,1,0:T(2,128)(2,1)S(1)}, u32[]{:S(2)}, u32[]{:S(2)}) collective-permute-start(bf16[3,2,1024]{2,1,0:T(2,128)(2,1)S(1)} %slice.4), channel_id=1, source_target_pairs={{0,8},{8,16},{16,24},{24,32},{32,40},{40,48},{48,56},{56,64},{64,7... | collective-permute-start | bytes 36872 | tf_op jit(solution)/shard_map/ppermute | solution.py:415
  5.2 3.6 %first_pass.1 = (f32[16,8,128]{2,1,0:T(8,128)S(1)}, f32[256,8,128]{2,1,0:T(8,128)S(1)}, f32[256,8,128]{2,1,0:T(8,128)S(1)}, f32[32,8,128]{2,1,0:T(8,128)S(1)}, s32[4,8,128]{2,1,0:T(8,128)S(1)}) custom-call(s32[4]{0:T(128)} %lengths_hbm.1, bf16[3,256,1024]{2,1,0:T(8,128)(2,1)} %bitcast.11, f32[3,3,1024]{2,1,0:T(4,128)} %taps_hbm.1, f32[16,1024]{1,0:T(8,128)} %rate_hbm.1), custom_call_target="tpu_custom_call" | custom-call | tf_op jit(solution)/shard_map/first_pass/pallas_call | solution.py:417
  8.9 0.0 collective-permute-done.edge_ref
  8.9 0.0 copy-done
  8.9 0.0 copy-done.1
  8.9 2.6 %edge_pass.1 = (f32[16,8,128]{2,1,0:T(8,128)S(1)}, f32[4,8,128]{2,1,0:T(8,128)S(1)}, f32[256,8,128]{2,1,0:T(8,128)S(1)}, f32[16,8,128]{2,1,0:T(8,128)S(1)}) custom-call(s32[4,8,128]{2,1,0:T(8,128)S(1)} %get-tuple-element.16.marks_ref, bf16[3,2,1024]{2,1,0:T(2,128)(2,1)S(1)} %collective-permute-done.edge_ref, f32[32,8,128]{2,1,0:T(8,128)S(1)} %get-tuple-element.17.consts_ref, ...), custom_call_target="tpu_custom_call" | custom-call | tf_op jit(solution)/shard_map/edge_pass/pallas_call | solution.py:434
  11.6 23.3 %all_to_all.26.ends_ref = f32[16,8,128]{2,1,0:T(8,128)S(1)} all-to-all(f32[16,8,128]{2,1,0:T(8,128)S(1)} %get-tuple-element.20), channel_id=1, replica_groups=mesh['row'=4,'far'=8,'near'=4,'chan'=8] {'row','near'}, dimensions={0} | all-to-all | bytes 131072 | tf_op jit(solution)/shard_map/all_to_all | solution.py:438
  34.9 0.1 block_totals.1
  35.0 38.6 %all_to_all.27.totals_ref = f32[32,8,128]{2,1,0:T(8,128)S(1)} all-to-all(f32[32,8,128]{2,1,0:T(8,128)S(1)} %block_totals.1), channel_id=1, replica_groups=mesh['row'=4,'far'=8,'near'=4,'chan'=8] {'far'}, dimensions={0} | all-to-all | bytes 262144 | tf_op jit(solution)/shard_map/all_to_all | solution.py:443
  73.6 0.2 spread_carry.1
  73.7 11.4 %all_to_all.28.arrived_ref = f32[16,8,128]{2,1,0:T(8,128)S(1)} all-to-all(f32[16,8,128]{2,1,0:T(8,128)S(1)} %spread_carry.1), channel_id=1, replica_groups=mesh['row'=4,'far'=8,'near'=4,'chan'=8] {'row','near'}, dimensions={0} | all-to-all | bytes 131072 | tf_op jit(solution)/shard_map/all_to_all | solution.py:447
  85.1 0.0 copy-start.2
  85.1 2.1 %second_pass.1 = (f32[256,1024]{1,0:T(8,128)S(1)}, f32[16,128]{1,0:T(8,128)S(1)}) custom-call(s32[4,8,128]{2,1,0:T(8,128)S(1)} %get-tuple-element.16.marks_ref, f32[16,8,128]{2,1,0:T(8,128)S(1)} %all_to_all.28.arrived_ref, f32[4,8,128]{2,1,0:T(8,128)S(1)} %get-tuple-element.21.head_ref, f32[256,8,128]{2,1,0:T(8,128)S(1)} %get-tuple-element.22.local_ref, ...), custom_call_target="tpu_custom_call" | custom-call | tf_op jit(solution)/shard_map/second_pass/pallas_call | solution.py:448
  87.2 15.3 %all_to_all.29 = f32[8,2,128]{2,1,0:T(2,128)S(1)} all-to-all(f32[8,2,128]{2,1,0:T(2,128)S(1)} %bitcast.8), channel_id=1, replica_groups=mesh['row'=4,'far'=8,'near'=4,'chan'=8] {'chan'}, dimensions={0} | all-to-all | bytes 16384 | tf_op jit(solution)/shard_map/all_to_all | solution.py:452
  102.5 0.0 copy-done.2
  102.5 1.2 %last_pass.1 = bf16[256,1024]{1,0:T(8,128)(2,1)} custom-call(f32[16,128]{1,0:T(8,128)S(1)} %bitcast.5, f32[256,1024]{1,0:T(8,128)S(1)} %get-tuple-element.26.response_ref, f32[1,1024]{1,0:T(1,128)S(1)} %bitcast.9), custom_call_target="tpu_custom_call" | custom-call | tf_op jit(solution)/shard_map/last_pass/pallas_call | solution.py:453
Async XLA Ops:
  0.0 8.9 %copy-start = (f32[16,1024]{1,0:T(8,128)S(1)}, f32[16,1024]{1,0:T(8,128)}, u32[]{:S(2)}) copy-start(f32[16,1024]{1,0:T(8,128)} %residue_ref.3) | copy-start | bytes 196612
  0.0 8.9 %copy-start.1 = (f32[1024]{0:T(1024)S(1)}, f32[1024]{0:T(1024)}, u32[]{:S(2)}) copy-start(f32[1024]{0:T(1024)} %param.11) | copy-start | bytes 12292
  0.9 8.0 %collective-permute-start = (bf16[3,2,1024]{2,1,0:T(2,128)(2,1)S(1)}, bf16[3,2,1024]{2,1,0:T(2,128)(2,1)S(1)}, u32[]{:S(2)}, u32[]{:S(2)}) collective-permute-start(bf16[3,2,1024]{2,1,0:T(2,128)(2,1)S(1)} %slice.4), channel_id=1, source_target_pairs={{0,8},{8,16},{16,24},{24,32},{32,40},{40,48},{48,56},{56,64},{64,7... | collective-permute-start | bytes 36872 | tf_op jit(solution)/shard_map/ppermute | solution.py:415
  85.1 17.4 %copy-start.2 = (f32[1024]{0:T(1024)S(1)}, f32[1024]{0:T(1024)}, u32[]{:S(2)}) copy-start(f32[1024]{0:T(1024)} %param.12) | copy-start | bytes 12292

commit v5 on v4

--- a/solution.py
+++ b/solution.py
@@ -13,7 +13,6 @@
 PAD = 8
 PIECES = 2
 CTX = ("row", "far", "near")
-HIGH = lax.Precision.HIGHEST
 
 
 def starts_of(lengths, anchor):
@@ -297,6 +296,14 @@
     lax.fori_loop(0, product_ref.shape[0] // CHUNK, chunk, 0)
 
 
+def in_thirds(value, axis):
+    high = value.astype(jnp.bfloat16)
+    rest = value - high.astype(jnp.float32)
+    middle = rest.astype(jnp.bfloat16)
+    low = (rest - middle.astype(jnp.float32)).astype(jnp.bfloat16)
+    return jnp.concatenate([high, middle, low], axis)
+
+
 def second_pass(marks_ref, arrived_ref, head_ref, local_ref, gains_ref, product_ref, query_ref, consts_ref,
                 residue_ref, skip_ref, response_ref, squares_ref, spread, states_ref, residue_rows):
     toks, sub, lanes = product_ref.shape
@@ -357,8 +364,8 @@
         response_ref[:, tile * lanes : (tile + 1) * lanes] = part
         total = total + part * part
     sums = lax.dot_general(
-        jnp.ones((squares_ref.shape[0], lanes), jnp.float32), total, (((1,), (1,)), ((), ())),
-        precision=HIGH, preferred_element_type=jnp.float32,
+        jnp.ones((squares_ref.shape[0], 3 * lanes), jnp.bfloat16), in_thirds(total, 1), (((1,), (1,)), ((), ())),
+        preferred_element_type=jnp.float32,
     )
     halves = toks // lanes
     half = lax.broadcasted_iota(jnp.int32, squares_ref.shape, 0) % halves
@@ -371,11 +378,12 @@
 def last_pass(squares_ref, response_ref, gain_ref, out_ref):
     count, lanes = squares_ref.shape
     halves = out_ref.shape[0] // lanes
-    half = lax.broadcasted_iota(jnp.int32, (count, lanes), 0) % halves
+    half = lax.broadcasted_iota(jnp.int32, (3 * count, lanes), 0) % halves
+    parts = in_thirds(squares_ref[...], 0)
     for h in range(halves):
         sums = lax.dot_general(
-            squares_ref[...], (half == h).astype(jnp.float32), (((0,), (0,)), ((), ())),
-            precision=HIGH, preferred_element_type=jnp.float32,
+            parts, (half == h).astype(jnp.bfloat16), (((0,), (0,)), ((), ())),
+            preferred_element_type=jnp.float32,
         )
         scale = lax.rsqrt(sums / D + eps_norm)
         toks = slice(h * lanes, (h + 1) * lanes)

time: 104 us -> 104 us (level)
  no operation moved by 1% of the time
where the time goes in v5:
time: 104 us
  blocking collectives  88.5 us (85%)
  Pallas kernels  9.73 us (9%)
  starting transfers between devices  4.37 us (4%)
    all_to_all x1, blocking collectives, shards(): totals = lax.all_to_all(totals, 'far', 0, 0, tiled=True)  38.5 us
    all_to_all x1, blocking collectives, shards(): ends = lax.all_to_all(ends, ('row', 'near'), 0, 0, tiled=True)  23.3 us
    all_to_all x1, blocking collectives, shards(): squares = lax.all_to_all(squares, 'chan', 0, 0, tiled=True)  15.2 us
    all_to_all x1, blocking collectives, shards(): arrived = lax.all_to_all(arrived, ('row', 'near'), 0, 0, tiled=True)  11.4 us
    ppermute x1, starting transfers between devices, shards(): lax.ppermute(parts[:, toks - 2:], CTX, [(i, i + 1) for i in range(count -...  4.37 us
    pallas_call x1, Pallas kernels, shards(): call(first_pass, 'aaaa', (tile(poles), tile(toks), tile(toks), tile(poles...  3.65 us
    pallas_call x1, Pallas kernels, shards(): call(edge_pass, 'vvvvvvv', (tile(poles), tile(4), tile(toks), tile(poles)...  2.65 us
    pallas_call x1, Pallas kernels, shards(): call(second_pass, 'vvvvvvvvvv', (flat(toks, channels), flat(wide * toks /...  2.11 us
  transfers between devices with their start and end apart: 1, of which 0 were waited for; matrix products, arithmetic and copies ran while one was open for 0% of the time, Pallas kernels for 4%

profile of v5, /device:TPU:1, one launch (start us, length us, event | category | flops | bytes accessed | tf_op | source)
XLA Modules:
  0.0 103.5 jit_solution(12889171053169764824)
XLA Ops:
  0.0 0.0 copy-start
  0.0 0.0 copy-start.1
  0.0 0.8 slice.4
  0.9 4.4 %collective-permute-start = (bf16[3,2,1024]{2,1,0:T(2,128)(2,1)S(1)}, bf16[3,2,1024]{2,1,0:T(2,128)(2,1)S(1)}, u32[]{:S(2)}, u32[]{:S(2)}) collective-permute-start(bf16[3,2,1024]{2,1,0:T(2,128)(2,1)S(1)} %slice.4), channel_id=1, source_target_pairs={{0,8},{8,16},{16,24},{24,32},{32,40},{40,48},{48,56},{56,64},{64,7... | collective-permute-start | bytes 36872 | tf_op jit(solution)/shard_map/ppermute | solution.py:423
  5.2 3.6 %first_pass.1 = (f32[16,8,128]{2,1,0:T(8,128)S(1)}, f32[256,8,128]{2,1,0:T(8,128)S(1)}, f32[256,8,128]{2,1,0:T(8,128)S(1)}, f32[32,8,128]{2,1,0:T(8,128)S(1)}, s32[4,8,128]{2,1,0:T(8,128)S(1)}) custom-call(s32[4]{0:T(128)} %lengths_hbm.1, bf16[3,256,1024]{2,1,0:T(8,128)(2,1)} %bitcast.11, f32[3,3,1024]{2,1,0:T(4,128)} %taps_hbm.1, f32[16,1024]{1,0:T(8,128)} %rate_hbm.1), custom_call_target="tpu_custom_call" | custom-call | tf_op jit(solution)/shard_map/first_pass/pallas_call | solution.py:425
  8.9 0.0 collective-permute-done.edge_ref
  8.9 0.0 copy-done
  8.9 0.0 copy-done.1
  8.9 2.6 %edge_pass.1 = (f32[16,8,128]{2,1,0:T(8,128)S(1)}, f32[4,8,128]{2,1,0:T(8,128)S(1)}, f32[256,8,128]{2,1,0:T(8,128)S(1)}, f32[16,8,128]{2,1,0:T(8,128)S(1)}) custom-call(s32[4,8,128]{2,1,0:T(8,128)S(1)} %get-tuple-element.16.marks_ref, bf16[3,2,1024]{2,1,0:T(2,128)(2,1)S(1)} %collective-permute-done.edge_ref, f32[32,8,128]{2,1,0:T(8,128)S(1)} %get-tuple-element.17.consts_ref, ...), custom_call_target="tpu_custom_call" | custom-call | tf_op jit(solution)/shard_map/edge_pass/pallas_call | solution.py:442
  11.6 23.3 %all_to_all.26.ends_ref = f32[16,8,128]{2,1,0:T(8,128)S(1)} all-to-all(f32[16,8,128]{2,1,0:T(8,128)S(1)} %get-tuple-element.20), channel_id=1, replica_groups=mesh['row'=4,'far'=8,'near'=4,'chan'=8] {'row','near'}, dimensions={0} | all-to-all | bytes 131072 | tf_op jit(solution)/shard_map/all_to_all | solution.py:446
  34.9 0.1 block_totals.1
  35.0 38.5 %all_to_all.27.totals_ref = f32[32,8,128]{2,1,0:T(8,128)S(1)} all-to-all(f32[32,8,128]{2,1,0:T(8,128)S(1)} %block_totals.1), channel_id=1, replica_groups=mesh['row'=4,'far'=8,'near'=4,'chan'=8] {'far'}, dimensions={0} | all-to-all | bytes 262144 | tf_op jit(solution)/shard_map/all_to_all | solution.py:451
  73.5 0.2 spread_carry.1
  73.7 11.4 %all_to_all.28.arrived_ref = f32[16,8,128]{2,1,0:T(8,128)S(1)} all-to-all(f32[16,8,128]{2,1,0:T(8,128)S(1)} %spread_carry.1), channel_id=1, replica_groups=mesh['row'=4,'far'=8,'near'=4,'chan'=8] {'row','near'}, dimensions={0} | all-to-all | bytes 131072 | tf_op jit(solution)/shard_map/all_to_all | solution.py:455
  85.0 0.0 copy-start.2
  85.0 2.1 %second_pass.1 = (f32[256,1024]{1,0:T(8,128)S(1)}, f32[16,128]{1,0:T(8,128)S(1)}) custom-call(s32[4,8,128]{2,1,0:T(8,128)S(1)} %get-tuple-element.16.marks_ref, f32[16,8,128]{2,1,0:T(8,128)S(1)} %all_to_all.28.arrived_ref, f32[4,8,128]{2,1,0:T(8,128)S(1)} %get-tuple-element.21.head_ref, f32[256,8,128]{2,1,0:T(8,128)S(1)} %get-tuple-element.22.local_ref, ...), custom_call_target="tpu_custom_call" | custom-call | tf_op jit(solution)/shard_map/second_pass/pallas_call | solution.py:456
  87.2 15.2 %all_to_all.29 = f32[8,2,128]{2,1,0:T(2,128)S(1)} all-to-all(f32[8,2,128]{2,1,0:T(2,128)S(1)} %bitcast.8), channel_id=1, replica_groups=mesh['row'=4,'far'=8,'near'=4,'chan'=8] {'chan'}, dimensions={0} | all-to-all | bytes 16384 | tf_op jit(solution)/shard_map/all_to_all | solution.py:460
  102.4 0.0 copy-done.2
  102.4 1.1 %last_pass.1 = bf16[256,1024]{1,0:T(8,128)(2,1)} custom-call(f32[16,128]{1,0:T(8,128)S(1)} %bitcast.5, f32[256,1024]{1,0:T(8,128)S(1)} %get-tuple-element.26.response_ref, f32[1,1024]{1,0:T(1,128)S(1)} %bitcast.9), custom_call_target="tpu_custom_call" | custom-call | tf_op jit(solution)/shard_map/last_pass/pallas_call | solution.py:461
Async XLA Ops:
  0.0 8.9 %copy-start = (f32[16,1024]{1,0:T(8,128)S(1)}, f32[16,1024]{1,0:T(8,128)}, u32[]{:S(2)}) copy-start(f32[16,1024]{1,0:T(8,128)} %residue_ref.3) | copy-start | bytes 196612
  0.0 8.9 %copy-start.1 = (f32[1024]{0:T(1024)S(1)}, f32[1024]{0:T(1024)}, u32[]{:S(2)}) copy-start(f32[1024]{0:T(1024)} %param.11) | copy-start | bytes 12292
  0.9 8.0 %collective-permute-start = (bf16[3,2,1024]{2,1,0:T(2,128)(2,1)S(1)}, bf16[3,2,1024]{2,1,0:T(2,128)(2,1)S(1)}, u32[]{:S(2)}, u32[]{:S(2)}) collective-permute-start(bf16[3,2,1024]{2,1,0:T(2,128)(2,1)S(1)} %slice.4), channel_id=1, source_target_pairs={{0,8},{8,16},{16,24},{24,32},{32,40},{40,48},{48,56},{56,64},{64,7... | collective-permute-start | bytes 36872 | tf_op jit(solution)/shard_map/ppermute | solution.py:423
  85.0 17.4 %copy-start.2 = (f32[1024]{0:T(1024)S(1)}, f32[1024]{0:T(1024)}, u32[]{:S(2)}) copy-start(f32[1024]{0:T(1024)} %param.12) | copy-start | bytes 12292
